TPU v7x, 512 devices: a whole 4x8x8 slice. The times are simulated.
512 devices in a mesh: mem: 64 (over y_hi, x, z), lat: 8 (over y_lo, core).
Axes of the slice: x: 4, y: 8 (y_hi: 2, y_lo: 4; y = y_hi * 4 + y_lo), z: 8, core: 2. Of those that a mesh axis runs over, the one named last changes fastest.
Arguments:
- ensemble: bfloat16 [64, 512, 3072], P('mem', 'lat'), may hold values from -0.75 to 0.75
- alpha: float32 [64, 512, 3072], P('mem', 'lat'), may hold values from -6 to 6
- background: float32 [512, 3072], P('lat'), may hold values from -4 to 4
- east_coef: float32 [512, 3072], P('lat'), may hold values from 0.03 to 0.24
- north_coef: float32 [512, 3072], P('lat'), may hold values from 0.03 to 0.24
- obs_cell: int32 [32768], P('lat'), may hold values from 0 to 1572863, as said below
- obs_type: int32 [32768], P('lat'), may hold values from 0 to 2
- obs_value: float32 [32768], P('lat'), may hold values from -5 to 5
- obs_weight: float32 [32768], P('lat'), may hold values from 1 to 8
Outputs:
- gradient: float32 [64, 512, 3072], P('mem', 'lat')
Inputs may be any that keep to these rules, and one draw needn't show every extreme that they name: `obs_cell`: observation i lies in latitude row (i // 4096) * 64 + (i % 4096) // 64; its column is arbitrary, and a cell may hold several observations.
All inputs are finite; a program needn't handle non-finite values.
Results may differ from a plain program's by a relative error of at most 0.0003.
Values sent between devices are 32-bit elements; how exact they have to be, the bound alone decides.
A program may use at most 64 MiB of HBM per device.

v0:
```python
import jax
import jax.numpy as jnp
from jax import lax
from jax.sharding import PartitionSpec as P

PASSES = 4


def extended_2(value, sides, width):
    for axis, dim in sides:
        size, length = (lax.axis_size(axis), value.shape[dim])
        up = [(i, (i + 1) % size) for i in range(size - 1)]
        down = [(j, i) for i, j in up]
        last = lax.slice_in_dim(value, length - width, length, axis=dim)
        first = lax.slice_in_dim(value, 0, width, axis=dim)
        before = lax.ppermute(last, axis, up)
        after = lax.ppermute(first, axis, down)
        value = jnp.concatenate([before, value, after], axis=dim)
    return value


def copy_for_each(value, axis):
    size = lax.axis_size(axis)
    return lax.all_to_all(
        jnp.broadcast_to(value[None], (size, *value.shape)), axis, 0, 0, tiled=True
    )


def over_copies(value, axis):
    return copy_for_each(value, axis).sum(axis=0)


def diffuse(field, east_coef, north_coef, south_coef, above, below):
    to_east = jnp.roll(field, -1, axis=1)
    to_west = jnp.roll(field, 1, axis=1)
    west_coef = jnp.roll(east_coef, 1, axis=1)
    return (
        field
        + east_coef * (to_east - field)
        + west_coef * (to_west - field)
        + north_coef * (above - field)
        + south_coef * (below - field)
    )


def deep_pass(field, coefs):
    east_ext, north_ext, south_ext, valid_rows = coefs
    extended = extended_2(field, (("lat", 0),), PASSES)
    zero_row = jnp.zeros_like(extended[:1])
    for repeat in range(PASSES):
        above = jnp.concatenate([extended[1:], zero_row], 0)
        below = jnp.concatenate([zero_row, extended[:-1]], 0)
        extended = valid_rows * diffuse(extended, east_ext, north_ext, south_ext, above, below)
    return extended[PASSES : extended.shape[0] - PASSES]


def observe(at_obs, obs_type, obs_value, obs_weight):
    mapped = jnp.where(
        obs_type == 0,
        at_obs,
        jnp.where(
            obs_type == 1, 0.5 * at_obs * jnp.abs(at_obs), 0.5 * jax.nn.softplus(2.0 * at_obs)
        ),
    )
    slope = jnp.where(
        obs_type == 0,
        jnp.ones_like(at_obs),
        jnp.where(obs_type == 1, jnp.abs(at_obs), jax.nn.sigmoid(2.0 * at_obs)),
    )
    return obs_weight * (mapped - obs_value) * slope


def pick_cells(field, obs_cols):
    safe_cols = jnp.clip(obs_cols, 0, field.shape[1] - 1)
    return jnp.take_along_axis(field, safe_cols, axis=1)


def spread_cells(values, obs_cols, width):
    rows = values.shape[0]
    row_ids = lax.broadcasted_iota(jnp.int32, values.shape, 0)
    return jnp.zeros((rows, width), jnp.float32).at[row_ids, obs_cols].add(values)


def per_device(
    ensemble, alpha, background, east_coef, north_coef, obs_cell, obs_type, obs_value, obs_weight
):
    slab_rows = background.shape[0]
    columns = background.shape[1]
    per_row = obs_cell.shape[0] // slab_rows
    zero_row = jnp.zeros_like(background[:1])
    stacked = jnp.stack([east_coef, north_coef])
    coef_ext = extended_2(stacked, (("lat", 1),), PASSES)
    east_ext = coef_ext[0]
    north_ext = coef_ext[1]
    south_ext = jnp.concatenate([zero_row, north_ext[:-1]], 0)
    global_row = (
        lax.axis_index("lat") * slab_rows
        - PASSES
        + lax.broadcasted_iota(jnp.int32, (slab_rows + 2 * PASSES, 1), 0)
    )
    valid_rows = ((global_row >= 0) & (global_row < slab_rows * lax.axis_size("lat"))).astype(
        jnp.float32
    )
    coefs = (east_ext, north_ext, south_ext, valid_rows)
    member = ensemble[0].astype(jnp.float32)
    control = alpha[0]
    member_term = member * deep_pass(control, coefs)
    obs_cols = (obs_cell % columns).reshape(slab_rows, per_row)
    obs_kind = obs_type.reshape(slab_rows, per_row)
    obs_target = obs_value.reshape(slab_rows, per_row)
    obs_scale = obs_weight.reshape(slab_rows, per_row)
    own_picked = pick_cells(member_term, obs_cols)
    picked = over_copies(own_picked, "mem")
    at_obs = pick_cells(background, obs_cols) + picked
    misfit = observe(at_obs, obs_kind, obs_target, obs_scale)
    forcing = spread_cells(misfit, obs_cols, columns)
    gradient = deep_pass(member * forcing, coefs) + control
    return gradient[None]


def solution(mesh):
    return jax.shard_map(
        per_device,
        mesh=mesh,
        in_specs=(
            P("mem", "lat", None),
            P("mem", "lat", None),
            P("lat", None),
            P("lat", None),
            P("lat", None),
            P("lat"),
            P("lat"),
            P("lat"),
            P("lat"),
        ),
        out_specs=P("mem", "lat", None),
        check_vma=False,
    )
```

profile of v0, /device:TPU:1, one launch (start us, length us, event | category | flops | bytes accessed | tf_op | source)
XLA Modules:
  0.0 169.9 jit_solution(824601750602922719)
XLA Ops:
  0.0 1.2 pad_maximum_fusion.5
  1.2 4.6 %collective-permute-start.2 = (f32[2,4,3072]{2,1,0:T(4,128)S(1)}, f32[2,4,3072]{2,1,0:T(4,128)S(1)}, u32[]{:S(2)}, u32[]{:S(2)}) collective-permute-start(f32[2,4,3072]{2,1,0:T(4,128)S(1)} %get-tuple-element.10), channel_id=1, source_target_pairs={{0,1},{1,2},{2,3},{3,4},{4,5},{5,6},{6,7},{8,9},{9,10},{10,11},{11... | collective-permute-start | bytes 294920 | tf_op jit(solution)/shard_map/ppermute | solution.py:16
  5.8 5.5 %collective-permute-start.3 = (f32[2,4,3072]{2,1,0:T(4,128)S(1)}, f32[2,4,3072]{2,1,0:T(4,128)}, u32[]{:S(2)}, u32[]{:S(2)}) collective-permute-start(f32[2,4,3072]{2,1,0:T(4,128)S(1)} %get-tuple-element.11), channel_id=1, source_target_pairs={{1,0},{2,1},{3,2},{4,3},{5,4},{6,5},{7,6},{9,8},{10,9},{11,10},{12... | collective-permute-start | bytes 294920 | tf_op jit(solution)/shard_map/ppermute | solution.py:17
  12.2 1.9 %collective-permute-start = (f32[4,3072]{1,0:T(4,128)S(1)}, f32[4,3072]{1,0:T(4,128)S(1)}, u32[]{:S(2)}, u32[]{:S(2)}) collective-permute-start(f32[4,3072]{1,0:T(4,128)S(1)} %get-tuple-element.62), channel_id=1, source_target_pairs={{0,1},{1,2},{2,3},{3,4},{4,5},{5,6},{6,7},{8,9},{9,10},{10,11},{11... | collective-permute-start | bytes 147464 | tf_op jit(solution)/shard_map/ppermute | solution.py:16
  14.1 2.4 %collective-permute-start.1 = (f32[4,3072]{1,0:T(4,128)S(1)}, f32[4,3072]{1,0:T(4,128)S(1)}, u32[]{:S(2)}, u32[]{:S(2)}) collective-permute-start(f32[4,3072]{1,0:T(4,128)S(1)} %get-tuple-element.63), channel_id=1, source_target_pairs={{1,0},{2,1},{3,2},{4,3},{5,4},{6,5},{7,6},{9,8},{10,9},{11,10},{12... | collective-permute-start | bytes 147464 | tf_op jit(solution)/shard_map/ppermute | solution.py:17
  17.6 2.0 %collective-permute-done.1 = f32[4,3072]{1,0:T(4,128)S(1)} collective-permute-done((f32[4,3072]{1,0:T(4,128)S(1)}, f32[4,3072]{1,0:T(4,128)S(1)}, u32[]{:S(2)}, u32[]{:S(2)}) %collective-permute-start.1) | collective-permute-done | bytes 49184 | tf_op jit(solution)/shard_map/ppermute | solution.py:17
  21.2 1.1 pad_maximum_fusion
  28.0 1.1 convert_multiply_fusion.1
  29.1 32.8 %gather_fusion.1 = f32[4096]{0:T(1024)S(1)} fusion(f32[64,3072]{1,0:T(8,128)S(1)} %convert_multiply_fusion.1, s32[4096]{0:T(1024)S(1)} %reshape.122), kind=kCustom, calls=%fused_computation.1.clone | custom fusion | bytes 65536 | tf_op jit(solution)/shard_map/jit(take_along_axis)/gather | solution.py:75
  62.0 1.6 broadcast_in_dim.18
  63.7 3.5 %reshape.133 = f32[64,1,4096]{2,1,0:T(1,128)} reshape(f32[64,64,64]{2,1,0:T(8,128)} %broadcast_in_dim.18) | data formatting | bytes 2097152
  67.1 16.5 %all-to-all-start = ((f32[64,1,4096]{2,1,0:T(1,128)}), f32[64,1,4096]{2,1,0:T(1,128)}, u32[]{:S(2)}, u32[]{:S(2)}) async-start(f32[64,1,4096]{2,1,0:T(1,128)} %reshape.133), calls=%async_computation | async-start | bytes 2097152 | tf_op jit(solution)/shard_map/all_to_all | solution.py:24
  83.7 32.8 %gather_fusion = f32[4096]{0:T(1024)S(1)} fusion(f32[64,3072]{1,0:T(8,128)S(1)} %copy-done, s32[4096]{0:T(1024)S(1)} %reshape.122), kind=kCustom, calls=%fused_computation.clone | custom fusion | bytes 65536 | tf_op jit(solution)/shard_map/jit(take_along_axis)/gather | solution.py:75
  117.8 5.4 %reduce.4 = f32[64,4096]{1,0:T(8,128)} reduce(f32[64,1,4096]{2,1,0:T(1,128)} %all-to-all-done, f32[]{:T(128)} %broadcast.190), dimensions={1}, to_apply=%all_to_all.3.reduce_sub_computation | reduce | bytes 2097156 | tf_op jit(solution)/shard_map/all_to_all | solution.py:24
  123.2 3.1 %reshape.134 = f32[64,64,64]{2,1,0:T(8,128)} reshape(f32[64,4096]{1,0:T(8,128)} %reduce.4) | data formatting | bytes 2097152
  126.3 1.8 %reduce_sum.9 = f32[64,64]{1,0:T(8,128)S(1)} reduce(f32[64,64,64]{2,1,0:T(8,128)} %reshape.134, f32[]{:T(128)} %constant.25.clone.1), dimensions={0}, to_apply=%region_0.2 | reduce | flops 258048 | bytes 1064964 | tf_op jit(solution)/shard_map/reduce_sum | solution.py:30
  128.2 22.1 %scatter_custom_fusion = f32[196608]{0:T(1024)S(1)} fusion(s32[4096]{0:T(1024)S(1)} %reshape.105, f32[4096]{0:T(1024)S(1)} %reshape.107, f32[]{:T(128)} %constant.25.clone.1), kind=kCustom, calls=%fused_computation.103 | custom fusion | flops 4096 | bytes 786436
  150.3 1.0 reshape.90
  151.3 1.3 convert_multiply_fusion
  152.7 2.2 %collective-permute-start.4 = (f32[4,3072]{1,0:T(4,128)S(1)}, f32[4,3072]{1,0:T(4,128)S(1)}, u32[]{:S(2)}, u32[]{:S(2)}) collective-permute-start(f32[4,3072]{1,0:T(4,128)S(1)} %get-tuple-element.60), channel_id=1, source_target_pairs={{0,1},{1,2},{2,3},{3,4},{4,5},{5,6},{6,7},{8,9},{9,10},{10,11},{11... | collective-permute-start | bytes 147464 | tf_op jit(solution)/shard_map/ppermute | solution.py:16
  154.8 2.2 %collective-permute-start.5 = (f32[4,3072]{1,0:T(4,128)S(1)}, f32[4,3072]{1,0:T(4,128)S(1)}, u32[]{:S(2)}, u32[]{:S(2)}) collective-permute-start(f32[4,3072]{1,0:T(4,128)S(1)} %get-tuple-element.61), channel_id=1, source_target_pairs={{1,0},{2,1},{3,2},{4,3},{5,4},{6,5},{7,6},{9,8},{10,9},{11,10},{12... | collective-permute-start | bytes 147464 | tf_op jit(solution)/shard_map/ppermute | solution.py:17
  157.0 3.2 %collective-permute-done.5 = f32[4,3072]{1,0:T(4,128)S(1)} collective-permute-done((f32[4,3072]{1,0:T(4,128)S(1)}, f32[4,3072]{1,0:T(4,128)S(1)}, u32[]{:S(2)}, u32[]{:S(2)}) %collective-permute-start.5) | collective-permute-done | bytes 49184 | tf_op jit(solution)/shard_map/ppermute | solution.py:17
  166.6 1.0 copy-done.6
  167.9 2.0 %fusion.51 = f32[1,64,3072]{2,1,0:T(8,128)} fusion(f32[72,1]{1,0:T(8,128)S(1)} %get-tuple-element.15, f32[72,3071]{1,0:T(8,128)S(1)} %get-tuple-element.13, f32[71,3072]{1,0:T(8,128)S(1)} %get-tuple-element.17, f32[71,3072]{1,0:T(8,128)S(1)} %get-tuple-element.16, f32[72,3072]{1,0:T(8,128)S(1)} %maximum_subtract_fusion.13, f32[72,3072]{1,0:T(8,128)S(1)} %fusion.40, ...), kind=kLoop, calls=%fused_computation.83 | loop fusion | flops 2949120 | bytes 9105664 | tf_op jit(solution)/shard_map/broadcast_in_dim | solution.py:118
  (103 shorter events, 17.1 us)
Async XLA Ops:
  0.0 83.6 %copy-start = (f32[64,3072]{1,0:T(8,128)S(1)}, f32[64,3072]{1,0:T(8,128)}, u32[]{:S(2)}) copy-start(f32[64,3072]{1,0:T(8,128)} %param.13) | copy-start | bytes 2359300
  0.0 19.6 %copy-start.5 = (f32[1,64,3072]{2,1,0:T(8,128)S(1)}, f32[1,64,3072]{2,1,0:T(8,128)}, u32[]{:S(2)}) copy-start(f32[1,64,3072]{2,1,0:T(8,128)} %param.12) | copy-start | bytes 2359300
  1.2 19.0 %collective-permute-start.2 = (f32[2,4,3072]{2,1,0:T(4,128)S(1)}, f32[2,4,3072]{2,1,0:T(4,128)S(1)}, u32[]{:S(2)}, u32[]{:S(2)}) collective-permute-start(f32[2,4,3072]{2,1,0:T(4,128)S(1)} %get-tuple-element.10), channel_id=1, source_target_pairs={{0,1},{1,2},{2,3},{3,4},{4,5},{5,6},{6,7},{8,9},{9,10},{10,11},{11... | collective-permute-start | bytes 294920 | tf_op jit(solution)/shard_map/ppermute | solution.py:16
  5.8 15.1 %collective-permute-start.3 = (f32[2,4,3072]{2,1,0:T(4,128)S(1)}, f32[2,4,3072]{2,1,0:T(4,128)}, u32[]{:S(2)}, u32[]{:S(2)}) collective-permute-start(f32[2,4,3072]{2,1,0:T(4,128)S(1)} %get-tuple-element.11), channel_id=1, source_target_pairs={{1,0},{2,1},{3,2},{4,3},{5,4},{6,5},{7,6},{9,8},{10,9},{11,10},{12... | collective-permute-start | bytes 294920 | tf_op jit(solution)/shard_map/ppermute | solution.py:17
  12.2 5.3 %collective-permute-start = (f32[4,3072]{1,0:T(4,128)S(1)}, f32[4,3072]{1,0:T(4,128)S(1)}, u32[]{:S(2)}, u32[]{:S(2)}) collective-permute-start(f32[4,3072]{1,0:T(4,128)S(1)} %get-tuple-element.62), channel_id=1, source_target_pairs={{0,1},{1,2},{2,3},{3,4},{4,5},{5,6},{6,7},{8,9},{9,10},{10,11},{11... | collective-permute-start | bytes 147464 | tf_op jit(solution)/shard_map/ppermute | solution.py:16
  14.1 5.4 %collective-permute-start.1 = (f32[4,3072]{1,0:T(4,128)S(1)}, f32[4,3072]{1,0:T(4,128)S(1)}, u32[]{:S(2)}, u32[]{:S(2)}) collective-permute-start(f32[4,3072]{1,0:T(4,128)S(1)} %get-tuple-element.63), channel_id=1, source_target_pairs={{1,0},{2,1},{3,2},{4,3},{5,4},{6,5},{7,6},{9,8},{10,9},{11,10},{12... | collective-permute-start | bytes 147464 | tf_op jit(solution)/shard_map/ppermute | solution.py:17
  19.8 1.1 copy-start.9
  19.8 1.4 copy-start.10
  22.5 4.7 %copy-start.1 = (f32[72,3072]{1,0:T(8,128)}, f32[72,3072]{1,0:T(8,128)S(1)}, u32[]{:S(2)}) copy-start(f32[72,3072]{1,0:T(8,128)S(1)} %get-tuple-element.9) | copy-start | bytes 2654212
  22.5 4.7 %copy-start.7 = (f32[72,3072]{1,0:T(8,128)}, f32[72,3072]{1,0:T(8,128)S(1)}, u32[]{:S(2)}) copy-start(f32[72,3072]{1,0:T(8,128)S(1)} %get-tuple-element.8) | copy-start | bytes 2654212
  22.6 4.6 %copy-start.3 = (f32[71,3072]{1,0:T(8,128)}, f32[71,3072]{1,0:T(8,128)S(1)}, u32[]{:S(2)}) copy-start(f32[71,3072]{1,0:T(8,128)S(1)} %slice_bitcast_fusion) | copy-start | bytes 2617348
  27.0 1.0 copy-start.11
  67.1 50.2 %all-to-all-start = ((f32[64,1,4096]{2,1,0:T(1,128)}), f32[64,1,4096]{2,1,0:T(1,128)}, u32[]{:S(2)}, u32[]{:S(2)}) async-start(f32[64,1,4096]{2,1,0:T(1,128)} %reshape.133), calls=%async_computation | async-start | bytes 2097152 | tf_op jit(solution)/shard_map/all_to_all | solution.py:24
  83.6 33.0 %copy-start.15 = (s32[4096]{0:T(1024)S(1)}, s32[4096]{0:T(1024)}, u32[]{:S(2)}) copy-start(s32[4096]{0:T(1024)} %param.17) | copy-start | bytes 49156
  83.6 33.1 %copy-start.13 = (f32[4096]{0:T(1024)S(1)}, f32[4096]{0:T(1024)}, u32[]{:S(2)}) copy-start(f32[4096]{0:T(1024)} %param.19) | copy-start | bytes 49156
  83.7 33.2 %copy-start.14 = (f32[4096]{0:T(1024)S(1)}, f32[4096]{0:T(1024)}, u32[]{:S(2)}) copy-start(f32[4096]{0:T(1024)} %param.18) | copy-start | bytes 49156
  83.7 33.4 %copy-start.17 = (s32[2]{0:T(128)S(1)}, s32[2]{0:T(128)}, u32[]{:S(2)}) copy-start(s32[2]{0:T(128)} %constant.92) | copy-start | bytes 28
  83.7 33.4 %copy-start.16 = (s32[2]{0:T(128)S(1)}, s32[2]{0:T(128)}, u32[]{:S(2)}) copy-start(s32[2]{0:T(128)} %constant.95) | copy-start | bytes 28
  152.7 4.3 %collective-permute-start.4 = (f32[4,3072]{1,0:T(4,128)S(1)}, f32[4,3072]{1,0:T(4,128)S(1)}, u32[]{:S(2)}, u32[]{:S(2)}) collective-permute-start(f32[4,3072]{1,0:T(4,128)S(1)} %get-tuple-element.60), channel_id=1, source_target_pairs={{0,1},{1,2},{2,3},{3,4},{4,5},{5,6},{6,7},{8,9},{9,10},{10,11},{11... | collective-permute-start | bytes 147464 | tf_op jit(solution)/shard_map/ppermute | solution.py:16
  154.8 5.4 %collective-permute-start.5 = (f32[4,3072]{1,0:T(4,128)S(1)}, f32[4,3072]{1,0:T(4,128)S(1)}, u32[]{:S(2)}, u32[]{:S(2)}) collective-permute-start(f32[4,3072]{1,0:T(4,128)S(1)} %get-tuple-element.61), channel_id=1, source_target_pairs={{1,0},{2,1},{3,2},{4,3},{5,4},{6,5},{7,6},{9,8},{10,9},{11,10},{12... | collective-permute-start | bytes 147464 | tf_op jit(solution)/shard_map/ppermute | solution.py:17
  160.5 1.2 copy-start.2
  160.5 1.4 copy-start.4
  166.5 1.1 copy-start.6
  166.5 1.4 copy-start.8
  (1 other events, 0.7 us)
where the time goes:
time: 171 us; the launch traced here: 170 us
  local copies, waits for them, and re-layouts  86 us (50%)
  other arithmetic  43 us (25%)
  starting transfers between devices  35.2 us (21%)
  waiting for transfers between devices  5.24 us (3%)
    gather x5, local copies, waits for them, and re-layouts, pick_cells(): return jnp.take_along_axis(field, safe_cols, axis=1)  65.9 us
    unnamed x4, other arithmetic  22.3 us
    all_to_all x1, starting transfers between devices, copy_for_each(): lax.all_to_all(jnp.broadcast_to(value[None], (size, *value.shape)), axis,...  16.5 us
    unnamed x39, local copies, waits for them, and re-layouts  10.8 us
    ppermute x3, starting transfers between devices, extended_2(): after = lax.ppermute(first, axis, down)  10 us
    ppermute x3, starting transfers between devices, extended_2(): before = lax.ppermute(last, axis, up)  8.67 us
    mul x6, other arithmetic, deep_pass(): valid_rows * diffuse(extended, east_ext, north_ext, south_ext, above, below)  5.57 us
    all_to_all x1, other arithmetic, copy_for_each(): lax.all_to_all(jnp.broadcast_to(value[None], (size, *value.shape)), axis,...  5.38 us
  transfers between devices with their start and end apart: 7, of which 2 were waited for; matrix products, arithmetic and copies ran while one was open for 21% of the time, Pallas kernels for 0%

commit v1 on v0

v1 whole, which is shorter than its diff:
```python
import functools

import jax
import jax.numpy as jnp
from jax import lax
from jax.experimental import pallas as pl
from jax.experimental.pallas import tpu as pltpu
from jax.sharding import PartitionSpec as P

PASSES = 4
AXES = (("y", 2), ("x", 4), ("z", 8))
ORDERS = ("zxy", "xyz", "yzx", "zyx")
LANES = 128
MESH = pl.DeviceIdType.MESH


def iota(shape, dim):
    return lax.broadcasted_iota(jnp.int32, shape, dim)


def lane_gather(values, lanes):
    return jnp.take_along_axis(values, lanes, axis=1, mode="promise_in_bounds")


def kernel(
    axes, alpha_hbm, member_hbm, back_hbm, east_hbm, north_hbm, cell_hbm, kind_hbm, value_hbm, weight_hbm,
    out_ref,
    field, east, north, ping, pong, member, back,
    cell_raw, kind_raw, value_raw, weight_raw, rows_int, rows_float,
    col_tile, key_tile, wgt_tile, wv_tile, sums, member_at, back_at, rep_tile, inverse,
    col_up, col_down, use_tile, use_up, use_down, part, inbox,
    load_sem, halo_send, halo_recv, stage_send, stage_recv,
):
    rows = alpha_hbm.shape[1]
    columns = alpha_hbm.shape[2]
    blocks = columns // LANES
    own = rows // 8
    half = own // 2
    per_row = LANES // 2
    lat = lax.axis_index("lat")
    lats = lax.axis_size("lat")
    mem = lax.axis_index("mem")
    has_up = lat < lats - 1
    has_down = lat > 0

    place = {}
    stride = {}
    rest = mem
    step = 1
    for name, size in reversed(axes):
        place[name] = lax.rem(rest, size)
        stride[name] = step
        rest = rest // size
        step = step * size
    sizes = dict(axes)

    def peer(name, ahead):
        there = lax.rem(place[name] + ahead, sizes[name])
        return {"mem": mem + (there - place[name]) * stride[name], "lat": lat}

    up = {"mem": mem, "lat": lat + 1}
    down = {"mem": mem, "lat": lat - 1}

    barrier = pltpu.get_barrier_semaphore()
    met = 0
    for name, size in axes:
        for ahead in range(1, size):
            pl.semaphore_signal(barrier, inc=1, device_id=peer(name, ahead), device_id_type=MESH)
            met += 1

    @pl.when(has_up)
    def _():
        pl.semaphore_signal(barrier, inc=1, device_id=up, device_id_type=MESH)

    @pl.when(has_down)
    def _():
        pl.semaphore_signal(barrier, inc=1, device_id=down, device_id_type=MESH)

    loads = [
        pltpu.make_async_copy(source, target, load_sem.at[index])
        for index, (source, target) in enumerate((
            (cell_hbm, cell_raw), (kind_hbm, kind_raw), (value_hbm, value_raw), (weight_hbm, weight_raw),
            (member_hbm.at[0], member), (alpha_hbm.at[0], field.at[pl.ds(0, rows)]),
            (east_hbm, east.at[pl.ds(0, rows)]), (north_hbm, north.at[pl.ds(0, rows)]), (back_hbm, back),
        ))
    ]
    for load in loads:
        load.start()

    tile = (8, LANES)
    lane = iota(tile, 1)
    sub = iota(tile, 0)
    low = lane < per_row

    zeros4 = jnp.zeros((4, columns), jnp.float32)

    @pl.when(jnp.logical_not(has_up))
    def _():
        for ref in (field, east, north):
            ref[rows : rows + 4, :] = zeros4
        col_up[...] = jnp.zeros(tile, jnp.int32)
        use_up[...] = jnp.zeros(tile, jnp.float32)

    @pl.when(jnp.logical_not(has_down))
    def _():
        for ref in (field, east, north):
            ref[rows + 4 : rows + 8, :] = zeros4
        col_down[...] = jnp.zeros(tile, jnp.int32)
        use_down[...] = jnp.zeros(tile, jnp.float32)

    def to_tiles(raw):
        rows_of = rows_int if raw.dtype == jnp.int32 else rows_float
        rows_of[pl.ds(0, rows // 2, stride=2), :] = raw
        rows_of[pl.ds(1, rows // 2, stride=2), :] = pltpu.roll(raw, per_row, 1)
        out = []
        for t in range(half):
            first = rows_of[8 * t : 8 * t + 8, :]
            second = rows_of[8 * (own - 1 - t) : 8 * (own - t), :]
            out.append(jnp.where(low, first, pltpu.roll(second, per_row, 1)))
        return out

    for load in loads[:4]:
        load.wait()
    raw_shape = (rows // 2, LANES)
    row_at = lat * rows + 2 * iota(raw_shape, 0) + iota(raw_shape, 1) // per_row
    col_raw = cell_raw[...] - row_at * columns
    weight = weight_raw[...]
    for t, value in enumerate(to_tiles(col_raw)):
        col_tile[t] = value
    for t, value in enumerate(to_tiles(col_raw * 4 + kind_raw[...])):
        key_tile[t] = value
    for t, value in enumerate(to_tiles(weight)):
        wgt_tile[t] = value
    for t, value in enumerate(to_tiles(weight * value_raw[...])):
        wv_tile[t] = value

    los = [col_tile[t] & (LANES - 1) for t in range(half)]
    his = [lax.shift_right_logical(col_tile[t], 7) for t in range(half)]

    def pick(j, accs, tiles):
        out = []
        for t in range(half):
            got = jnp.where(low, lane_gather(tiles[t], los[t]), lane_gather(tiles[own - 1 - t], los[t]))
            out.append(jnp.where(his[t] == j, got, accs[t]))
        return tuple(out)

    def block(j):
        return pl.ds(pl.multiple_of(j * LANES, LANES), LANES)

    zero_tiles = tuple(jnp.zeros(tile, jnp.float32) for _ in range(half))
    loads[4].wait()

    def pick_member(j, accs):
        pairs = [member[16 * k : 16 * k + 16, block(j)].astype(jnp.float32) for k in range(half)]
        tiles = [pair[8 * side : 8 * side + 8] for pair in pairs for side in range(2)]
        return pick(j, accs, tiles)

    for t, value in enumerate(lax.fori_loop(0, blocks, pick_member, zero_tiles)):
        member_at[t] = value

    pl.semaphore_wait(barrier, met + has_up.astype(jnp.int32) + has_down.astype(jnp.int32))

    def halo(index, source, target, device):
        return pltpu.make_async_remote_copy(
            src_ref=source, dst_ref=target, send_sem=halo_send.at[index], recv_sem=halo_recv.at[index],
            device_id=device, device_id_type=MESH,
        )

    sources = (alpha_hbm.at[0], east_hbm, north_hbm)
    targets = (field, east, north)
    to_up = [
        halo(i, s.at[pl.ds(rows - 4, 4)], t.at[pl.ds(rows + 4, 4)], up)
        for i, (s, t) in enumerate(zip(sources, targets))
    ] + [halo(3, col_tile.at[0], col_down, up)]
    to_down = [
        halo(4 + i, s.at[pl.ds(0, 4)], t.at[pl.ds(rows, 4)], down)
        for i, (s, t) in enumerate(zip(sources, targets))
    ] + [halo(7, col_tile.at[0], col_up, down)]

    @pl.when(has_up)
    def _():
        for copy in to_up:
            copy.start()

    @pl.when(has_down)
    def _():
        for copy in to_down:
            copy.start()

    loads[8].wait()

    def pick_back(j, accs):
        return pick(j, accs, [back[8 * t : 8 * t + 8, block(j)] for t in range(own)])

    for t, value in enumerate(lax.fori_loop(0, blocks, pick_back, zero_tiles)):
        back_at[t] = value

    for load in loads[5:8]:
        load.wait()

    @pl.when(has_up)
    def _():
        for copy in to_down:
            copy.wait_recv()

    @pl.when(has_down)
    def _():
        for copy in to_up:
            copy.wait_recv()

    keep = jnp.where((sub >= 4) | has_up, 1.0, 0.0)
    last_lane = lane == LANES - 1
    first_lane = lane == 0
    last_sub = sub == 7
    first_sub = sub == 0
    count = own + 1

    def get(ref, t, j):
        return ref[8 * t : 8 * t + 8, block(j)]

    def diffuse(source, finish, init=()):
        first = [get(source, t, 0) for t in range(count)]
        rolled = tuple(pltpu.roll(v, LANES - 1, 1) for v in first)
        from_west = []
        for t in range(count):
            v = get(source, t, blocks - 1)
            flux = get(east, t, blocks - 1) * (jnp.where(last_lane, rolled[t], pltpu.roll(v, LANES - 1, 1)) - v)
            from_west.append(pltpu.roll(flux, 1, 1))

        def body(j, carry):
            rolled, from_west, extra = carry
            after = lax.rem(j + 1, blocks)
            vs = [get(source, t, j) for t in range(count)]
            lifted = [pltpu.roll(v, 7, 0) for v in vs]
            rise = []
            for t in range(count):
                above = jnp.where(last_sub, lifted[(t + 1) % count], lifted[t])
                rise.append(get(north, t, j) * (above - vs[t]))
            sunk = [pltpu.roll(f, 1, 0) for f in rise]
            next_rolled, next_west, results = [], [], []
            for t in range(count):
                ahead = pltpu.roll(get(source, t, after), LANES - 1, 1)
                flux = get(east, t, j) * (jnp.where(last_lane, ahead, rolled[t]) - vs[t])
                turned = pltpu.roll(flux, 1, 1)
                west = jnp.where(first_lane, from_west[t], turned)
                south = jnp.where(first_sub, sunk[t - 1], sunk[t])
                result = vs[t] + ((flux - west) + (rise[t] - south))
                results.append(result * keep if t == own else result)
                next_rolled.append(ahead)
                next_west.append(turned)
            return tuple(next_rolled), tuple(next_west), finish(j, results, extra)

        return lax.fori_loop(0, blocks, body, (rolled, tuple(from_west), init))[2]

    def into(target):
        def finish(j, results, extra):
            for t in range(count):
                target[8 * t : 8 * t + 8, block(j)] = results[t]
            return extra

        return finish

    diffuse(field, into(ping))
    diffuse(ping, into(pong))
    diffuse(pong, into(ping))
    picked = diffuse(ping, lambda j, results, accs: pick(j, accs, results), zero_tiles)
    for t in range(half):
        part[t] = member_at[t] * picked[t]

    def stage_copy(t, stage, index, ahead, slot):
        name = ORDERS[t % len(ORDERS)][stage]
        return pltpu.make_async_remote_copy(
            src_ref=part.at[stage * half + t], dst_ref=inbox.at[slot],
            send_sem=stage_send.at[slot], recv_sem=stage_recv.at[slot],
            device_id=peer(name, ahead), device_id_type=MESH,
        )

    copies = []
    slot = 0
    for t in range(half):
        of_tile = []
        for stage in range(3):
            of_stage = []
            for ahead in range(1, sizes[ORDERS[t % len(ORDERS)][stage]]):
                of_stage.append((stage_copy(t, stage, 0, ahead, slot), slot))
                slot += 1
            of_tile.append(of_stage)
        copies.append(of_tile)

    def send(t, stage):
        for copy, _ in copies[t][stage]:
            copy.start()

    def collect(t, stage):
        total = part[stage * half + t]
        for copy, at in copies[t][stage]:
            copy.wait_recv()
            total = total + inbox[at]
        return total

    for t in range(half):
        send(t, 0)

    half_base = lane & per_row
    in_half = lane & (per_row - 1)
    for t in range(half):
        key = key_tile[t]
        col = col_tile[t]
        wgt = wgt_tile[t]
        wv = wv_tile[t]
        kind = key & 3

        def merge(d, carry, col=col, key=key, wgt=wgt, wv=wv):
            w0, w1, w2, v0, v1, v2, repeat = carry
            lanes = half_base | ((lane - d) & (per_row - 1))
            other = lane_gather(key, lanes)
            w = lane_gather(wgt, lanes)
            v = lane_gather(wv, lanes)
            same = lax.shift_right_logical(other, 2) == col
            kind = other & 3
            m0 = same & (kind == 0)
            m1 = same & (kind == 1)
            m2 = same & (kind == 2)
            return (
                w0 + jnp.where(m0, w, 0.0), w1 + jnp.where(m1, w, 0.0), w2 + jnp.where(m2, w, 0.0),
                v0 + jnp.where(m0, v, 0.0), v1 + jnp.where(m1, v, 0.0), v2 + jnp.where(m2, v, 0.0),
                jnp.where(same & (in_half >= d), 1, repeat),
            )

        init = tuple(jnp.where(kind == k, wgt, 0.0) for k in range(3)) + tuple(
            jnp.where(kind == k, wv, 0.0) for k in range(3)
        ) + (jnp.zeros(tile, jnp.int32),)
        merged = lax.fori_loop(1, per_row, merge, init)
        for k in range(6):
            sums[6 * t + k] = merged[k]
        rep_tile[t] = jnp.where(merged[6] == 0, lane + 1, 0)

    for t in range(half):
        total = collect(t, 0)
        part[half + t] = total
        send(t, 1)

    halo_cols = jnp.where(sub < 4, col_up[...], col_down[...])
    col_tile[half] = halo_cols

    def find_repeat(d, repeat):
        lanes = half_base | ((lane - d) & (per_row - 1))
        return jnp.where((lane_gather(halo_cols, lanes) == halo_cols) & (in_half >= d), 1, repeat)

    repeat = lax.fori_loop(1, per_row, find_repeat, jnp.zeros(tile, jnp.int32))
    rep_tile[half] = jnp.where(repeat == 0, lane + 1, 0)

    def spot(t, s):
        col = col_tile[t, pl.ds(s, 1), :]
        rep = rep_tile[t, pl.ds(s, 1), :].astype(jnp.float32)
        hi = lax.shift_right_logical(col, 7)
        lo = col & (LANES - 1)
        ones = jnp.where(iota((LANES, LANES), 0) == lo, 1.0, 0.0).astype(jnp.bfloat16)
        at = jnp.where(iota((blocks, LANES), 0) == hi, rep, 0.0)
        right = iota((blocks, LANES), 1) < per_row
        split = jnp.concatenate([jnp.where(right, at, 0.0), jnp.where(right, 0.0, at)], axis=0).astype(jnp.bfloat16)
        return lax.dot_general(split, ones, (((1,), (1,)), ((), ())), preferred_element_type=jnp.float32)

    def own_rows(s, carry):
        for t in range(half):
            found = spot(t, s)
            inverse[t, pl.ds(s, blocks, stride=8), :] = found[:blocks]
            inverse[own - 1 - t, pl.ds(s, blocks, stride=8), :] = found[blocks:]
        return carry

    lax.fori_loop(0, 8, own_rows, 0)

    def halo_rows(s, carry):
        found = spot(half, s)
        inverse[own, pl.ds(s, blocks, stride=8), :] = jnp.where(s < 4, found[:blocks], found[blocks:])
        return carry

    lax.fori_loop(0, 8, halo_rows, 0)

    for t in range(half):
        total = collect(t, 1)
        part[2 * half + t] = total
        send(t, 2)

    uses = []
    for t in range(half):
        s = back_at[t] + collect(t, 2)
        w0, w1, w2, v0, v1, v2 = [sums[6 * t + k] for k in range(6)]
        size = jnp.abs(s)
        small = jnp.exp(-2.0 * size)
        soft = jnp.maximum(2.0 * s, 0.0) + jnp.log1p(small)
        slope = jnp.where(s >= 0, 1.0, small) / (1.0 + small)
        misfit = (w0 * s - v0) + (w1 * (0.5 * s * size) - v1) * size + (w2 * (0.5 * soft) - v2) * slope
        use = member_at[t] * misfit
        uses.append(use)
        use_tile[t] = use
        if t == 0:
            use_to_up = halo(8, use_tile.at[0], use_down, up)
            use_to_down = halo(9, use_tile.at[0], use_up, down)

            @pl.when(has_up)
            def _():
                use_to_up.start()

            @pl.when(has_down)
            def _():
                use_to_down.start()

    def place_tile(t, values):
        for j in range(blocks):
            found = inverse[t, 8 * j : 8 * j + 8, :].astype(jnp.int32)
            got = lane_gather(values, jnp.maximum(found - 1, 0))
            ping[8 * t : 8 * t + 8, j * LANES : (j + 1) * LANES] = jnp.where(found > 0, got, 0.0)

    for t in range(half):
        place_tile(t, uses[t])
        place_tile(own - 1 - t, uses[t])

    @pl.when(has_up)
    def _():
        use_to_down.wait_recv()

    @pl.when(has_down)
    def _():
        use_to_up.wait_recv()

    place_tile(own, jnp.where(sub < 4, use_up[...], use_down[...]))

    def to_out(j, results, extra):
        for t in range(own):
            out_ref[0, 8 * t : 8 * t + 8, block(j)] = results[t] + get(field, t, j)
        return extra

    diffuse(ping, into(pong))
    diffuse(pong, into(ping))
    diffuse(ping, into(pong))
    diffuse(pong, to_out)

    for of_tile in copies:
        for of_stage in of_tile:
            for copy, _ in of_stage:
                copy.wait_send()

    @pl.when(has_up)
    def _():
        for copy in to_up + [use_to_up]:
            copy.wait_send()

    @pl.when(has_down)
    def _():
        for copy in to_down + [use_to_down]:
            copy.wait_send()


def make(mesh, axes=AXES):
    def per_device(ensemble, alpha, background, east_coef, north_coef, obs_cell, obs_type, obs_value, obs_weight):
        rows, columns = background.shape
        blocks = columns // LANES
        own = rows // 8
        half = own // 2
        ext = rows + 8
        packed = (rows // 2, LANES)
        tile = (8, LANES)
        slots = half * sum(size - 1 for _, size in axes)
        f32, i32 = jnp.float32, jnp.int32
        VMEM = pltpu.VMEM
        scratch = [
            VMEM((ext, columns), f32), VMEM((ext, columns), f32), VMEM((ext, columns), f32),
            VMEM((ext, columns), f32), VMEM((ext, columns), f32),
            VMEM((rows, columns), jnp.bfloat16), VMEM((rows, columns), f32),
            VMEM(packed, i32), VMEM(packed, i32), VMEM(packed, f32), VMEM(packed, f32),
            VMEM((rows, LANES), i32), VMEM((rows, LANES), f32),
            VMEM((half + 1, *tile), i32), VMEM((half, *tile), i32), VMEM((half, *tile), f32), VMEM((half, *tile), f32),
            VMEM((6 * half, *tile), f32), VMEM((half, *tile), f32), VMEM((half, *tile), f32),
            VMEM((half + 1, *tile), i32), VMEM((own + 1, 8 * blocks, LANES), f32),
            VMEM(tile, i32), VMEM(tile, i32), VMEM((half, *tile), f32), VMEM(tile, f32), VMEM(tile, f32),
            VMEM((3 * half, *tile), f32), VMEM((slots, *tile), f32),
            pltpu.SemaphoreType.DMA((9,)), pltpu.SemaphoreType.DMA((10,)), pltpu.SemaphoreType.DMA((10,)),
            pltpu.SemaphoreType.DMA((slots,)), pltpu.SemaphoreType.DMA((slots,)),
        ]
        return pl.pallas_call(
            functools.partial(kernel, axes),
            out_shape=jax.ShapeDtypeStruct((1, rows, columns), f32),
            in_specs=[pl.BlockSpec(memory_space=pl.ANY)] * 9,
            out_specs=pl.BlockSpec(memory_space=pltpu.VMEM),
            scratch_shapes=scratch,
            compiler_params=pltpu.CompilerParams(collective_id=0, has_side_effects=True),
            name="gradient",
        )(
            alpha, ensemble, background, east_coef, north_coef,
            obs_cell.reshape(packed), obs_type.reshape(packed), obs_value.reshape(packed), obs_weight.reshape(packed),
        )

    return jax.shard_map(
        per_device,
        mesh=mesh,
        in_specs=(
            P("mem", "lat", None), P("mem", "lat", None), P("lat", None), P("lat", None), P("lat", None),
            P("lat"), P("lat"), P("lat"), P("lat"),
        ),
        out_specs=P("mem", "lat", None),
        check_vma=False,
    )


def solution(mesh):
    return make(mesh)
```

time: 171 us -> 90.1 us (0.53)
  Pallas kernels: 0 us -> 87.9 us
  local copies, waits for them, and re-layouts: 86 us -> 2.07 us
  other arithmetic: 43 us -> 0 us
  starting transfers between devices: 35.2 us -> 0 us
  waiting for transfers between devices: 5.24 us -> 0 us
    pallas_call x0 -> x1, Pallas kernels: none -> 87.9 us  [per_device(): pl.pallas_call(functools.partial(kernel, axes), out_shape=jax.ShapeDtypeS...]
    gather x5 -> x0, local copies, waits for them, and re-layouts: 65.9 us -> none  [pick_cells(): return jnp.take_along_axis(field, safe_cols, axis=1)]
    unnamed x4 -> x0, other arithmetic: 22.3 us -> none
    ppermute x6 -> x0, starting transfers between devices: 18.7 us -> none  [the longest x3 10 us: extended_2(): after = lax.ppermute(first, axis, down)]
    all_to_all x1 -> x0, starting transfers between devices: 16.5 us -> none  [copy_for_each(): lax.all_to_all(jnp.broadcast_to(value[None], (size, *value.shape)), axis,...]
    unnamed x39 -> x1, local copies, waits for them, and re-layouts: 10.8 us -> 2.07 us
    mul x9 -> x0, other arithmetic: 8.02 us -> none  [the longest x6 5.57 us: deep_pass(): valid_rows * diffuse(extended, east_ext, north_ext, south_ext, above, below)]
    slice x29 -> x0, local copies, waits for them, and re-layouts: 5.48 us -> none  [the longest x12 2.31 us: diffuse(): to_west = jnp.roll(field, 1, axis=1)]
  transfers between devices with their start and end apart: 7 -> 0, of which waited for: 2 -> 0; matrix products, arithmetic and copies ran while one was open for 21% -> 0% of each run, Pallas kernels for 0% -> 0%
where the time goes in v1:
time: 90.1 us; the launch traced here: 90 us
  Pallas kernels  87.9 us (98%)
  local copies, waits for them, and re-layouts  2.07 us (2%)
    pallas_call x1, Pallas kernels, per_device(): pl.pallas_call(functools.partial(kernel, axes), out_shape=jax.ShapeDtypeS...  87.9 us
    unnamed x1, local copies, waits for them, and re-layouts  2.07 us

profile of v1, /device:TPU:1, one launch (start us, length us, event | category | flops | bytes accessed | tf_op | source)
XLA Modules:
  0.0 90.0 jit_solution(15901275856513455014)
XLA Ops:
  0.0 87.9 %gradient.1 = f32[1,64,3072]{2,1,0:T(8,128)} custom-call(f32[1,64,3072]{2,1,0:T(8,128)} %alpha_hbm.1, bf16[1,64,3072]{2,1,0:T(8,128)(2,1)} %member_hbm.1, f32[64,3072]{1,0:T(8,128)} %back_hbm.1, f32[64,3072]{1,0:T(8,128)} %east_hbm.1, f32[64,3072]{1,0:T(8,128)} %north_hbm.1, s32[32,128]{1,0:T(8,128)} %bitcast.4, s32[32,128]{1,0:T(8,128)} %bitcast.5, ...), custom_call_target="tpu_custom_call" | custom-call | tf_op jit(solution)/shard_map/gradient/pallas_call | solution.py:481
  87.9 2.1 %copy.11 = f32[1,64,3072]{2,1,0:T(8,128)} copy(f32[1,64,3072]{2,1,0:T(8,128)} %gradient.1) | data formatting | bytes 1572864

commit v2 on v1

v2 whole, which is shorter than its diff:
```python
import functools
import itertools

import jax
import jax.numpy as jnp
from jax import lax
from jax.experimental import pallas as pl
from jax.experimental.pallas import tpu as pltpu
from jax.sharding import PartitionSpec as P

PASSES = 4
AXES = (("y", 2), ("x", 4), ("z", 8))
ORDERS = (("z", "xy"), ("xy", "z"), ("z", "xy"), ("xy", "z"))
HOPS = {"y": 4, "x": 1, "z": 1}
LANES = 128
UNROLL = 24
LIMIT = 20 * 2**20
MESH = pl.DeviceIdType.MESH


def iota(shape, dim):
    return lax.broadcasted_iota(jnp.int32, shape, dim)


def lane_gather(values, lanes):
    return jnp.take_along_axis(values, lanes, axis=1, mode="promise_in_bounds")


def kernel(
    axes, alpha_hbm, member_hbm, back_hbm, east_hbm, north_hbm, cell_hbm, kind_hbm, value_hbm, weight_hbm,
    out_ref,
    field, east, north, ping, pong, third, edge_a, edge_b, member, back,
    cell_raw, kind_raw, value_raw, weight_raw, rows_int, rows_float,
    col_tile, key_tile, wgt_tile, wv_tile, sums, member_at, back_at, rep_tile, inverse,
    col_up, col_down, use_tile, use_up, use_down, part, inbox,
    load_sem, halo_send, halo_recv, stage_send, stage_recv, relay,
):
    rows = alpha_hbm.shape[1]
    columns = alpha_hbm.shape[2]
    blocks = columns // LANES
    own = rows // 8
    half = own // 2
    unroll = UNROLL if blocks % UNROLL == 0 else 1
    per_row = LANES // 2
    lat = lax.axis_index("lat")
    lats = lax.axis_size("lat")
    mem = lax.axis_index("mem")
    has_up = lat < lats - 1
    has_down = lat > 0

    place = {}
    stride = {}
    rest = mem
    step = 1
    for name, size in reversed(axes):
        place[name] = lax.rem(rest, size)
        stride[name] = step
        rest = rest // size
        step = step * size
    sizes = dict(axes)

    def peer(move):
        to = mem
        for name, ahead in move:
            there = lax.rem(place[name] + ahead, sizes[name])
            to = to + (there - place[name]) * stride[name]
        return {"mem": to, "lat": lat}

    def hops(move):
        return sum(HOPS[name] * min(ahead, sizes[name] - ahead) for name, ahead in move)

    def moves(names):
        every = itertools.product(*[[(name, ahead) for ahead in range(sizes[name])] for name in names])
        return sorted((m for m in every if any(ahead for _, ahead in m)), key=hops, reverse=True)

    up = {"mem": mem, "lat": lat + 1}
    down = {"mem": mem, "lat": lat - 1}

    barrier = pltpu.get_barrier_semaphore()
    met = 0
    for name, size in axes:
        for move in moves(name):
            pl.semaphore_signal(barrier, inc=1, device_id=peer(move), device_id_type=MESH)
            met += 1

    @pl.when(has_up)
    def _():
        pl.semaphore_signal(barrier, inc=1, device_id=up, device_id_type=MESH)

    @pl.when(has_down)
    def _():
        pl.semaphore_signal(barrier, inc=1, device_id=down, device_id_type=MESH)

    loads = [
        pltpu.make_async_copy(source, target, load_sem.at[index])
        for index, (source, target) in enumerate((
            (cell_hbm, cell_raw), (kind_hbm, kind_raw), (value_hbm, value_raw), (weight_hbm, weight_raw),
            (member_hbm.at[0], member), (alpha_hbm.at[0], field.at[pl.ds(0, rows)]),
            (east_hbm, east.at[pl.ds(0, rows)]), (north_hbm, north.at[pl.ds(0, rows)]), (back_hbm, back),
        ))
    ]
    for load in loads:
        load.start()

    tile = (8, LANES)
    lane = iota(tile, 1)
    sub = iota(tile, 0)
    low = lane < per_row

    zeros4 = jnp.zeros((4, columns), jnp.float32)

    @pl.when(jnp.logical_not(has_up))
    def _():
        for ref in (field, east, north):
            ref[rows : rows + 4, :] = zeros4
        col_up[...] = jnp.zeros(tile, jnp.int32)
        use_up[...] = jnp.zeros(tile, jnp.float32)

    @pl.when(jnp.logical_not(has_down))
    def _():
        for ref in (field, east, north):
            ref[rows + 4 : rows + 8, :] = zeros4
        col_down[...] = jnp.zeros(tile, jnp.int32)
        use_down[...] = jnp.zeros(tile, jnp.float32)

    def to_tiles(raw):
        rows_of = rows_int if raw.dtype == jnp.int32 else rows_float
        rows_of[pl.ds(0, rows // 2, stride=2), :] = raw
        rows_of[pl.ds(1, rows // 2, stride=2), :] = pltpu.roll(raw, per_row, 1)
        out = []
        for t in range(half):
            first = rows_of[8 * t : 8 * t + 8, :]
            second = rows_of[8 * (own - 1 - t) : 8 * (own - t), :]
            out.append(jnp.where(low, first, pltpu.roll(second, per_row, 1)))
        return out

    for load in loads[:4]:
        load.wait()
    raw_shape = (rows // 2, LANES)
    row_at = lat * rows + 2 * iota(raw_shape, 0) + iota(raw_shape, 1) // per_row
    col_raw = cell_raw[...] - row_at * columns
    weight = weight_raw[...]
    for t, value in enumerate(to_tiles(col_raw)):
        col_tile[t] = value
    for t, value in enumerate(to_tiles(col_raw * 4 + kind_raw[...])):
        key_tile[t] = value
    for t, value in enumerate(to_tiles(weight)):
        wgt_tile[t] = value
    for t, value in enumerate(to_tiles(weight * value_raw[...])):
        wv_tile[t] = value

    los = [col_tile[t] & (LANES - 1) for t in range(half)]
    his = [lax.shift_right_logical(col_tile[t], 7) for t in range(half)]

    def pick(j, accs, tiles):
        out = []
        for t in range(half):
            got = jnp.where(low, lane_gather(tiles[t], los[t]), lane_gather(tiles[own - 1 - t], los[t]))
            out.append(jnp.where(his[t] == j, got, accs[t]))
        return tuple(out)

    def block(j):
        return pl.ds(pl.multiple_of(j * LANES, LANES), LANES)

    zero_tiles = tuple(jnp.zeros(tile, jnp.float32) for _ in range(half))

    def over_blocks(step):
        def body(i, accs):
            for u in range(unroll):
                accs = step(i * unroll + u, accs)
            return accs

        return lax.fori_loop(0, blocks // unroll, body, zero_tiles)

    loads[4].wait()

    def pick_member(j, accs):
        pairs = [member[16 * k : 16 * k + 16, block(j)].astype(jnp.float32) for k in range(half)]
        tiles = [pair[8 * side : 8 * side + 8] for pair in pairs for side in range(2)]
        return pick(j, accs, tiles)

    for t, value in enumerate(over_blocks(pick_member)):
        member_at[t] = value

    pl.semaphore_wait(barrier, met + has_up.astype(jnp.int32) + has_down.astype(jnp.int32))

    for move in moves("x"):
        pl.semaphore_signal(relay, inc=1, device_id=peer(move), device_id_type=MESH)

    def halo(index, source, target, device):
        return pltpu.make_async_remote_copy(
            src_ref=source, dst_ref=target, send_sem=halo_send.at[index], recv_sem=halo_recv.at[index],
            device_id=device, device_id_type=MESH,
        )

    sources = (alpha_hbm.at[0], east_hbm, north_hbm)
    targets = (field, east, north)
    to_up = [
        halo(i, s.at[pl.ds(rows - 4, 4)], t.at[pl.ds(rows + 4, 4)], up)
        for i, (s, t) in enumerate(zip(sources, targets))
    ] + [halo(3, col_tile.at[0], col_down, up)]
    to_down = [
        halo(4 + i, s.at[pl.ds(0, 4)], t.at[pl.ds(rows, 4)], down)
        for i, (s, t) in enumerate(zip(sources, targets))
    ] + [halo(7, col_tile.at[0], col_up, down)]

    @pl.when(has_up)
    def _():
        for copy in to_up:
            copy.start()

    @pl.when(has_down)
    def _():
        for copy in to_down:
            copy.start()

    for load in loads[5:8]:
        load.wait()

    keep = jnp.where((sub >= 4) | has_up, 1.0, 0.0)
    last_lane = lane == LANES - 1
    first_lane = lane == 0
    last_sub = sub == 7
    first_sub = sub == 0
    def get(ref, t, j):
        return ref[8 * t : 8 * t + 8, block(j)]

    def diffuse(source, tiles, coefs, finish, init=()):
        turn = LANES - 1
        ring = range(len(tiles))
        rolled = tuple(pltpu.roll(get(source, t, 0), turn, 1) for t in tiles)
        from_west = []
        for k in ring:
            v = get(source, tiles[k], blocks - 1)
            flux = get(east, coefs[k], blocks - 1) * (jnp.where(last_lane, rolled[k], pltpu.roll(v, turn, 1)) - v)
            from_west.append(pltpu.roll(flux, 1, 1))

        def body(i, carry):
            rolled, from_west, extra = carry
            for u in range(unroll):
                j = i * unroll + u
                after = j + 1
                if u == unroll - 1:
                    after = jnp.where(after == blocks, 0, after)
                vs = [get(source, t, j) for t in tiles]
                lifted = [pltpu.roll(v, 7, 0) for v in vs]
                rise = []
                for k in ring:
                    above = jnp.where(last_sub, lifted[(k + 1) % len(tiles)], lifted[k])
                    rise.append(get(north, coefs[k], j) * (above - vs[k]))
                sunk = [pltpu.roll(f, 1, 0) for f in rise]
                next_rolled, next_west, results = [], [], []
                for k in ring:
                    ahead = pltpu.roll(get(source, tiles[k], after), turn, 1)
                    flux = get(east, coefs[k], j) * (jnp.where(last_lane, ahead, rolled[k]) - vs[k])
                    turned = pltpu.roll(flux, 1, 1)
                    west = jnp.where(first_lane, from_west[k], turned)
                    south = jnp.where(first_sub, sunk[k - 1], sunk[k])
                    result = vs[k] + ((flux - west) + (rise[k] - south))
                    results.append(result * keep if coefs[k] == own else result)
                    next_rolled.append(ahead)
                    next_west.append(turned)
                rolled, from_west = tuple(next_rolled), tuple(next_west)
                extra = finish(j, results, extra)
            return rolled, from_west, extra

        return lax.fori_loop(0, blocks // unroll, body, (rolled, tuple(from_west), init))[2]

    def into(target):
        def finish(j, results, extra):
            for t, result in enumerate(results):
                target[8 * t : 8 * t + 8, block(j)] = result
            return extra

        return finish

    inner = list(range(own))
    edge = [own - 1, own, 0]
    flat = [0, 1, 2]
    from_edge = jnp.where(low, sub, 7 - sub) < 4

    diffuse(field, inner, inner, into(ping))
    diffuse(ping, inner, inner, into(pong))
    diffuse(pong, inner, inner, into(ping))
    picked = diffuse(ping, inner, inner, lambda j, results, accs: pick(j, accs, results), zero_tiles)
    for t in range(1, half):
        part[t] = member_at[t] * picked[t]

    def stage_copy(t, stage, move, slot):
        return pltpu.make_async_remote_copy(
            src_ref=part.at[stage * half + t], dst_ref=inbox.at[slot],
            send_sem=stage_send.at[slot], recv_sem=stage_recv.at[slot],
            device_id=peer(move), device_id_type=MESH,
        )

    copies = []
    slot = 0
    for t in range(half):
        of_tile = []
        for stage in range(2):
            of_stage = []
            for move in moves(ORDERS[t % len(ORDERS)][stage]):
                of_stage.append((stage_copy(t, stage, move, slot), slot))
                slot += 1
            of_tile.append(of_stage)
        copies.append(of_tile)

    def send(t, stage):
        for copy, _ in copies[t][stage]:
            copy.start()

    def collect(t, stage):
        total = part[stage * half + t]
        for copy, at in copies[t][stage]:
            copy.wait_recv()
            total = total + inbox[at]
        return total

    pl.semaphore_wait(relay, len(moves("x")))
    for t in range(1, half):
        send(t, 0)

    @pl.when(has_up)
    def _():
        for copy in to_down:
            copy.wait_recv()

    @pl.when(has_down)
    def _():
        for copy in to_up:
            copy.wait_recv()

    def pick_edge(j, results, acc):
        got = jnp.where(low, lane_gather(results[2], los[0]), lane_gather(results[0], los[0]))
        return jnp.where(his[0] == j, got, acc)

    diffuse(field, edge, edge, into(edge_a))
    diffuse(edge_a, flat, edge, into(edge_b))
    diffuse(edge_b, flat, edge, into(edge_a))
    picked_edge = diffuse(edge_a, flat, edge, pick_edge, zero_tiles[0])
    part[0] = member_at[0] * jnp.where(from_edge, picked_edge, picked[0])
    send(0, 0)

    half_base = lane & per_row
    in_half = lane & (per_row - 1)

    def merge(i, carry):
        carry = list(carry)
        for u in range(3):
            d = 3 * i + 1 + u
            lanes = half_base | ((lane - d) & (per_row - 1))
            later = in_half >= d
            for t in range(half):
                w0, w1, w2, v0, v1, v2, repeat = carry[t]
                other = lane_gather(key_tile[t], lanes)
                w = lane_gather(wgt_tile[t], lanes)
                v = lane_gather(wv_tile[t], lanes)
                same = lax.shift_right_logical(other, 2) == col_tile[t]
                kind = other & 3
                m0 = same & (kind == 0)
                m1 = same & (kind == 1)
                m2 = same & (kind == 2)
                carry[t] = (
                    w0 + jnp.where(m0, w, 0.0), w1 + jnp.where(m1, w, 0.0), w2 + jnp.where(m2, w, 0.0),
                    v0 + jnp.where(m0, v, 0.0), v1 + jnp.where(m1, v, 0.0), v2 + jnp.where(m2, v, 0.0),
                    jnp.where(same & later, 1, repeat),
                )
        return tuple(carry)

    start = []
    for t in range(half):
        kind = key_tile[t] & 3
        start.append(
            tuple(jnp.where(kind == k, wgt_tile[t], 0.0) for k in range(3))
            + tuple(jnp.where(kind == k, wv_tile[t], 0.0) for k in range(3))
            + (jnp.zeros(tile, jnp.int32),)
        )
    merged = lax.fori_loop(0, (per_row - 1) // 3, merge, tuple(start))
    for t in range(half):
        for k in range(6):
            sums[6 * t + k] = merged[t][k]
        rep_tile[t] = jnp.where(merged[t][6] == 0, lane + 1, 0)

    loads[8].wait()

    def pick_back(j, accs):
        return pick(j, accs, [back[8 * t : 8 * t + 8, block(j)] for t in range(own)])

    for t, value in enumerate(over_blocks(pick_back)):
        back_at[t] = value

    for t in range(1, half):
        total = collect(t, 0)
        part[half + t] = total
        send(t, 1)

    halo_cols = jnp.where(sub < 4, col_up[...], col_down[...])
    col_tile[half] = halo_cols

    def find_repeat(i, repeat):
        for u in range(9):
            d = 9 * i + 1 + u
            lanes = half_base | ((lane - d) & (per_row - 1))
            repeat = jnp.where((lane_gather(halo_cols, lanes) == halo_cols) & (in_half >= d), 1, repeat)
        return repeat

    repeat = lax.fori_loop(0, (per_row - 1) // 9, find_repeat, jnp.zeros(tile, jnp.int32))
    rep_tile[half] = jnp.where(repeat == 0, lane + 1, 0)

    def spot(t, s):
        col = col_tile[t, pl.ds(s, 1), :]
        rep = rep_tile[t, pl.ds(s, 1), :].astype(jnp.float32)
        hi = lax.shift_right_logical(col, 7)
        lo = col & (LANES - 1)
        ones = jnp.where(iota((LANES, LANES), 0) == lo, 1.0, 0.0).astype(jnp.bfloat16)
        at = jnp.where(iota((blocks, LANES), 0) == hi, rep, 0.0)
        right = iota((blocks, LANES), 1) < per_row
        split = jnp.concatenate([jnp.where(right, at, 0.0), jnp.where(right, 0.0, at)], axis=0).astype(jnp.bfloat16)
        return lax.dot_general(split, ones, (((1,), (1,)), ((), ())), preferred_element_type=jnp.float32)

    def all_rows(i, carry):
        for s in (2 * i, 2 * i + 1):
            for t in range(half):
                found = spot(t, s)
                inverse[t, pl.ds(s, blocks, stride=8), :] = found[:blocks]
                inverse[own - 1 - t, pl.ds(s, blocks, stride=8), :] = found[blocks:]
            found = spot(half, s)
            inverse[own, pl.ds(s, blocks, stride=8), :] = jnp.where(s < 4, found[:blocks], found[blocks:])
        return carry

    lax.fori_loop(0, 4, all_rows, 0)

    part[half] = collect(0, 0)
    send(0, 1)

    def use_of(t):
        s = back_at[t] + collect(t, 1)
        w0, w1, w2, v0, v1, v2 = [sums[6 * t + k] for k in range(6)]
        size = jnp.abs(s)
        small = jnp.exp(-2.0 * size)
        soft = jnp.maximum(2.0 * s, 0.0) + jnp.log1p(small)
        slope = jnp.where(s >= 0, 1.0, small) / (1.0 + small)
        misfit = (w0 * s - v0) + (w1 * (0.5 * s * size) - v1) * size + (w2 * (0.5 * soft) - v2) * slope
        return member_at[t] * misfit

    def place_tile(t, values):
        for j in range(blocks):
            found = inverse[t, 8 * j : 8 * j + 8, :].astype(jnp.int32)
            got = lane_gather(values, jnp.maximum(found - 1, 0))
            ping[8 * t : 8 * t + 8, j * LANES : (j + 1) * LANES] = jnp.where(found > 0, got, 0.0)

    for t in range(1, half):
        use = use_of(t)
        place_tile(t, use)
        place_tile(own - 1 - t, use)

    use = use_of(0)
    use_tile[0] = use
    use_to_up = halo(8, use_tile.at[0], use_down, up)
    use_to_down = halo(9, use_tile.at[0], use_up, down)

    @pl.when(has_up)
    def _():
        use_to_up.start()

    @pl.when(has_down)
    def _():
        use_to_down.start()

    place_tile(0, use)
    place_tile(own - 1, use)

    def to_out(j, results, extra):
        for t in range(own):
            out_ref[0, 8 * t : 8 * t + 8, block(j)] = results[t] + get(field, t, j)
        return extra

    def edge_out(j, results, extra):
        for k, t, mine in ((2, 0, sub < 4), (0, own - 1, sub >= 4)):
            rows_at = pl.ds(8 * t, 8)
            value = jnp.where(mine, results[k] + get(field, t, j), out_ref[0, rows_at, block(j)])
            out_ref[0, rows_at, block(j)] = value
        return extra

    diffuse(ping, inner, inner, into(pong))
    diffuse(pong, inner, inner, into(third))
    diffuse(third, inner, inner, into(pong))
    diffuse(pong, inner, inner, to_out)

    @pl.when(has_up)
    def _():
        use_to_down.wait_recv()

    @pl.when(has_down)
    def _():
        use_to_up.wait_recv()

    place_tile(own, jnp.where(sub < 4, use_up[...], use_down[...]))
    diffuse(ping, edge, edge, into(edge_a))
    diffuse(edge_a, flat, edge, into(edge_b))
    diffuse(edge_b, flat, edge, into(edge_a))
    diffuse(edge_a, flat, edge, edge_out)

    for of_tile in copies:
        for of_stage in of_tile:
            for copy, _ in of_stage:
                copy.wait_send()

    @pl.when(has_up)
    def _():
        for copy in to_up + [use_to_up]:
            copy.wait_send()

    @pl.when(has_down)
    def _():
        for copy in to_down + [use_to_down]:
            copy.wait_send()


def make(mesh, axes=AXES):
    def per_device(ensemble, alpha, background, east_coef, north_coef, obs_cell, obs_type, obs_value, obs_weight):
        rows, columns = background.shape
        blocks = columns // LANES
        own = rows // 8
        half = own // 2
        ext = rows + 8
        packed = (rows // 2, LANES)
        tile = (8, LANES)
        count = dict(axes)
        slots = half * (count["x"] * count["y"] + count["z"] - 2)
        f32, i32 = jnp.float32, jnp.int32
        VMEM = pltpu.VMEM
        scratch = [
            VMEM((ext, columns), f32), VMEM((ext, columns), f32), VMEM((ext, columns), f32),
            VMEM((ext, columns), f32), VMEM((ext, columns), f32), VMEM((rows, columns), f32),
            VMEM((24, columns), f32), VMEM((24, columns), f32),
            VMEM((rows, columns), jnp.bfloat16), VMEM((rows, columns), f32),
            VMEM(packed, i32), VMEM(packed, i32), VMEM(packed, f32), VMEM(packed, f32),
            VMEM((rows, LANES), i32), VMEM((rows, LANES), f32),
            VMEM((half + 1, *tile), i32), VMEM((half, *tile), i32), VMEM((half, *tile), f32), VMEM((half, *tile), f32),
            VMEM((6 * half, *tile), f32), VMEM((half, *tile), f32), VMEM((half, *tile), f32),
            VMEM((half + 1, *tile), i32), VMEM((own + 1, 8 * blocks, LANES), f32),
            VMEM(tile, i32), VMEM(tile, i32), VMEM((half, *tile), f32), VMEM(tile, f32), VMEM(tile, f32),
            VMEM((2 * half, *tile), f32), VMEM((slots, *tile), f32),
            pltpu.SemaphoreType.DMA((9,)), pltpu.SemaphoreType.DMA((10,)), pltpu.SemaphoreType.DMA((10,)),
            pltpu.SemaphoreType.DMA((slots,)), pltpu.SemaphoreType.DMA((slots,)), pltpu.SemaphoreType.REGULAR,
        ]
        return pl.pallas_call(
            functools.partial(kernel, axes),
            out_shape=jax.ShapeDtypeStruct((1, rows, columns), f32),
            in_specs=[pl.BlockSpec(memory_space=pltpu.HBM)] * 9,
            out_specs=pl.BlockSpec(memory_space=pltpu.VMEM),
            scratch_shapes=scratch,
            compiler_params=pltpu.CompilerParams(collective_id=0, has_side_effects=True, vmem_limit_bytes=LIMIT),
            name="gradient",
        )(*[pltpu.with_memory_space_constraint(a, pltpu.HBM) for a in (
            alpha, ensemble, background, east_coef, north_coef,
            obs_cell.reshape(packed), obs_type.reshape(packed), obs_value.reshape(packed), obs_weight.reshape(packed),
        )])

    return jax.shard_map(
        per_device,
        mesh=mesh,
        in_specs=(
            P("mem", "lat", None), P("mem", "lat", None), P("lat", None), P("lat", None), P("lat", None),
            P("lat"), P("lat"), P("lat"), P("lat"),
        ),
        out_specs=P("mem", "lat", None),
        check_vma=False,
    )


def solution(mesh):
    return make(mesh)
```

time: 90.1 us -> 39.5 us (0.44)
  Pallas kernels: 87.9 us -> 38.4 us
  local copies, waits for them, and re-layouts: 2.07 us -> 0.88 us
    pallas_call x1, Pallas kernels: 87.9 us -> 38.4 us  [per_device(): pl.pallas_call(functools.partial(kernel, axes), out_shape=jax.ShapeDtypeS...]
    unnamed x1, local copies, waits for them, and re-layouts: 2.07 us -> 0.88 us
where the time goes in v2:
time: 39.5 us; the launch traced here: 39.3 us
  Pallas kernels  38.4 us (97%)
  local copies, waits for them, and re-layouts  0.88 us (2%)
    pallas_call x1, Pallas kernels, per_device(): pl.pallas_call(functools.partial(kernel, axes), out_shape=jax.ShapeDtypeS...  38.4 us
    unnamed x1, local copies, waits for them, and re-layouts  0.88 us

profile of v2, /device:TPU:1, one launch (start us, length us, event | category | flops | bytes accessed | tf_op | source)
XLA Modules:
  0.0 39.3 jit_solution(9103276651856649363)
XLA Ops:
  0.0 38.4 %gradient.1 = f32[1,64,3072]{2,1,0:T(8,128)S(1)} custom-call(f32[1,64,3072]{2,1,0:T(8,128)} %alpha_hbm.1, bf16[1,64,3072]{2,1,0:T(8,128)(2,1)} %member_hbm.1, f32[64,3072]{1,0:T(8,128)} %back_hbm.1, f32[64,3072]{1,0:T(8,128)} %east_hbm.1, f32[64,3072]{1,0:T(8,128)} %north_hbm.1, s32[32,128]{1,0:T(8,128)} %bitcast.4, s32[32,128]{1,0:T(8,128)} %bitcast.5, ...), custom_call_target="tpu_custom_call" | custom-call | tf_op jit(solution)/shard_map/gradient/pallas_call | solution.py:548
  38.4 0.9 %copy.11 = f32[1,64,3072]{2,1,0:T(8,128)} copy(f32[1,64,3072]{2,1,0:T(8,128)S(1)} %gradient.1) | data formatting | bytes 1572864

commit v3 on v2

--- a/solution.py
+++ b/solution.py
@@ -13,7 +13,6 @@
 ORDERS = (("z", "xy"), ("xy", "z"), ("z", "xy"), ("xy", "z"))
 HOPS = {"y": 4, "x": 1, "z": 1}
 LANES = 128
-UNROLL = 24
 LIMIT = 20 * 2**20
 MESH = pl.DeviceIdType.MESH
 
@@ -29,7 +28,7 @@
 def kernel(
     axes, alpha_hbm, member_hbm, back_hbm, east_hbm, north_hbm, cell_hbm, kind_hbm, value_hbm, weight_hbm,
     out_ref,
-    field, east, north, ping, pong, third, edge_a, edge_b, member, back,
+    field, east, north, west, ping, pong, third, edge_a, edge_b, member, back,
     cell_raw, kind_raw, value_raw, weight_raw, rows_int, rows_float,
     col_tile, key_tile, wgt_tile, wv_tile, sums, member_at, back_at, rep_tile, inverse,
     col_up, col_down, use_tile, use_up, use_down, part, inbox,
@@ -40,8 +39,18 @@
     blocks = columns // LANES
     own = rows // 8
     half = own // 2
-    unroll = UNROLL if blocks % UNROLL == 0 else 1
     per_row = LANES // 2
+    loads = [
+        pltpu.make_async_copy(source, target, load_sem.at[index])
+        for index, (source, target) in enumerate((
+            (alpha_hbm.at[0], field.at[pl.ds(0, rows)]), (east_hbm, east.at[pl.ds(0, rows)]),
+            (north_hbm, north.at[pl.ds(0, rows)]), (cell_hbm, cell_raw), (kind_hbm, kind_raw),
+            (value_hbm, value_raw), (weight_hbm, weight_raw), (member_hbm.at[0], member), (back_hbm, back),
+        ))
+    ]
+    for load in loads:
+        load.start()
+
     lat = lax.axis_index("lat")
     lats = lax.axis_size("lat")
     mem = lax.axis_index("mem")
@@ -91,16 +100,37 @@
     def _():
         pl.semaphore_signal(barrier, inc=1, device_id=down, device_id_type=MESH)
 
-    loads = [
-        pltpu.make_async_copy(source, target, load_sem.at[index])
-        for index, (source, target) in enumerate((
-            (cell_hbm, cell_raw), (kind_hbm, kind_raw), (value_hbm, value_raw), (weight_hbm, weight_raw),
-            (member_hbm.at[0], member), (alpha_hbm.at[0], field.at[pl.ds(0, rows)]),
-            (east_hbm, east.at[pl.ds(0, rows)]), (north_hbm, north.at[pl.ds(0, rows)]), (back_hbm, back),
-        ))
+    pl.semaphore_wait(barrier, met + has_up.astype(jnp.int32) + has_down.astype(jnp.int32))
+
+    for move in moves("x"):
+        pl.semaphore_signal(relay, inc=1, device_id=peer(move), device_id_type=MESH)
+
+    def halo(index, source, target, device):
+        return pltpu.make_async_remote_copy(
+            src_ref=source, dst_ref=target, send_sem=halo_send.at[index], recv_sem=halo_recv.at[index],
+            device_id=device, device_id_type=MESH,
+        )
+
+    sources = (alpha_hbm.at[0], east_hbm, north_hbm)
+    targets = (field, east, north)
+    to_up = [
+        halo(i, s.at[pl.ds(rows - 4, 4)], t.at[pl.ds(rows + 4, 4)], up)
+        for i, (s, t) in enumerate(zip(sources, targets))
     ]
-    for load in loads:
-        load.start()
+    to_down = [
+        halo(4 + i, s.at[pl.ds(0, 4)], t.at[pl.ds(rows, 4)], down)
+        for i, (s, t) in enumerate(zip(sources, targets))
+    ]
+
+    @pl.when(has_up)
+    def _():
+        for copy in to_up:
+            copy.start()
+
+    @pl.when(has_down)
+    def _():
+        for copy in to_down:
+            copy.start()
 
     tile = (8, LANES)
     lane = iota(tile, 1)
@@ -122,6 +152,67 @@
             ref[rows + 4 : rows + 8, :] = zeros4
         col_down[...] = jnp.zeros(tile, jnp.int32)
         use_down[...] = jnp.zeros(tile, jnp.float32)
+
+    keep = jnp.where((sub >= 4) | has_up, 1.0, 0.0)
+    last_lane = lane == LANES - 1
+    first_lane = lane == 0
+    last_sub = sub == 7
+    first_sub = sub == 0
+
+    def block(j):
+        return slice(j * LANES, (j + 1) * LANES)
+
+    def get(ref, t, j):
+        return ref[8 * t : 8 * t + 8, block(j % blocks)]
+
+    def west_tile(t):
+        turned = [pltpu.roll(get(east, t, j), 1, 1) for j in range(blocks)]
+        for j in range(blocks):
+            west[8 * t : 8 * t + 8, block(j)] = jnp.where(first_lane, turned[j - 1], turned[j])
+
+    def diffuse(source, tiles, coefs, group, finish):
+        size = len(tiles)
+        for at in range(0, size, group):
+            mine = range(at, at + group)
+            near = list(mine) if group == size else [(at - 1) % size, *mine, (at + group) % size]
+            ahead = {k: pltpu.roll(get(source, tiles[k], 0), LANES - 1, 1) for k in mine}
+            behind = {k: pltpu.roll(get(source, tiles[k], -1), 1, 1) for k in mine}
+            for j in range(blocks):
+                vs = [get(source, tiles[k], j) for k in near]
+                lifted = [pltpu.roll(v, 7, 0) for v in vs]
+                rise = []
+                for i in range(len(near) if group == size else len(near) - 1):
+                    above = jnp.where(last_sub, lifted[(i + 1) % len(near)], lifted[i])
+                    rise.append(get(north, coefs[near[i]], j) * (above - vs[i]))
+                sunk = [pltpu.roll(f, 1, 0) for f in rise]
+                for i, k in enumerate(mine, 0 if group == size else 1):
+                    v = vs[i]
+                    turned_east = pltpu.roll(get(source, tiles[k], j + 1), LANES - 1, 1)
+                    turned_west = pltpu.roll(v, 1, 1)
+                    side = get(east, coefs[k], j) * (jnp.where(last_lane, turned_east, ahead[k]) - v)
+                    side = side + get(west, coefs[k], j) * (jnp.where(first_lane, behind[k], turned_west) - v)
+                    result = v + (side + (rise[i] - jnp.where(first_sub, sunk[i - 1], sunk[i])))
+                    finish(k, j, result * keep if coefs[k] == own else result)
+                    ahead[k], behind[k] = turned_east, turned_west
+
+    def into(target):
+        def finish(k, j, result):
+            target[8 * k : 8 * k + 8, block(j)] = result
+
+        return finish
+
+    inner = list(range(own))
+    edge = [own - 1, own, 0]
+    flat = [0, 1, 2]
+
+    for load in loads[:3]:
+        load.wait()
+    for t in range(own):
+        west_tile(t)
+    diffuse(field, inner, inner, half, into(ping))
+    diffuse(ping, inner, inner, half, into(pong))
+    diffuse(pong, inner, inner, half, into(ping))
+    diffuse(ping, inner, inner, half, into(pong))
 
     def to_tiles(raw):
         rows_of = rows_int if raw.dtype == jnp.int32 else rows_float
@@ -134,7 +225,7 @@
             out.append(jnp.where(low, first, pltpu.roll(second, per_row, 1)))
         return out
 
-    for load in loads[:4]:
+    for load in loads[3:7]:
         load.wait()
     raw_shape = (rows // 2, LANES)
     row_at = lat * rows + 2 * iota(raw_shape, 0) + iota(raw_shape, 1) // per_row
@@ -149,140 +240,42 @@
     for t, value in enumerate(to_tiles(weight * value_raw[...])):
         wv_tile[t] = value
 
+    cols_to_up = halo(3, col_tile.at[0], col_down, up)
+    cols_to_down = halo(7, col_tile.at[0], col_up, down)
+
+    @pl.when(has_up)
+    def _():
+        cols_to_up.start()
+
+    @pl.when(has_down)
+    def _():
+        cols_to_down.start()
+
     los = [col_tile[t] & (LANES - 1) for t in range(half)]
     his = [lax.shift_right_logical(col_tile[t], 7) for t in range(half)]
-
-    def pick(j, accs, tiles):
-        out = []
-        for t in range(half):
-            got = jnp.where(low, lane_gather(tiles[t], los[t]), lane_gather(tiles[own - 1 - t], los[t]))
-            out.append(jnp.where(his[t] == j, got, accs[t]))
-        return tuple(out)
-
-    def block(j):
-        return pl.ds(pl.multiple_of(j * LANES, LANES), LANES)
-
-    zero_tiles = tuple(jnp.zeros(tile, jnp.float32) for _ in range(half))
-
-    def over_blocks(step):
-        def body(i, accs):
-            for u in range(unroll):
-                accs = step(i * unroll + u, accs)
-            return accs
-
-        return lax.fori_loop(0, blocks // unroll, body, zero_tiles)
-
-    loads[4].wait()
-
-    def pick_member(j, accs):
-        pairs = [member[16 * k : 16 * k + 16, block(j)].astype(jnp.float32) for k in range(half)]
-        tiles = [pair[8 * side : 8 * side + 8] for pair in pairs for side in range(2)]
-        return pick(j, accs, tiles)
-
-    for t, value in enumerate(over_blocks(pick_member)):
-        member_at[t] = value
-
-    pl.semaphore_wait(barrier, met + has_up.astype(jnp.int32) + has_down.astype(jnp.int32))
-
-    for move in moves("x"):
-        pl.semaphore_signal(relay, inc=1, device_id=peer(move), device_id_type=MESH)
-
-    def halo(index, source, target, device):
-        return pltpu.make_async_remote_copy(
-            src_ref=source, dst_ref=target, send_sem=halo_send.at[index], recv_sem=halo_recv.at[index],
-            device_id=device, device_id_type=MESH,
-        )
-
-    sources = (alpha_hbm.at[0], east_hbm, north_hbm)
-    targets = (field, east, north)
-    to_up = [
-        halo(i, s.at[pl.ds(rows - 4, 4)], t.at[pl.ds(rows + 4, 4)], up)
-        for i, (s, t) in enumerate(zip(sources, targets))
-    ] + [halo(3, col_tile.at[0], col_down, up)]
-    to_down = [
-        halo(4 + i, s.at[pl.ds(0, 4)], t.at[pl.ds(rows, 4)], down)
-        for i, (s, t) in enumerate(zip(sources, targets))
-    ] + [halo(7, col_tile.at[0], col_up, down)]
-
-    @pl.when(has_up)
-    def _():
-        for copy in to_up:
-            copy.start()
-
-    @pl.when(has_down)
-    def _():
-        for copy in to_down:
-            copy.start()
-
-    for load in loads[5:8]:
-        load.wait()
-
-    keep = jnp.where((sub >= 4) | has_up, 1.0, 0.0)
-    last_lane = lane == LANES - 1
-    first_lane = lane == 0
-    last_sub = sub == 7
-    first_sub = sub == 0
-    def get(ref, t, j):
-        return ref[8 * t : 8 * t + 8, block(j)]
-
-    def diffuse(source, tiles, coefs, finish, init=()):
-        turn = LANES - 1
-        ring = range(len(tiles))
-        rolled = tuple(pltpu.roll(get(source, t, 0), turn, 1) for t in tiles)
-        from_west = []
-        for k in ring:
-            v = get(source, tiles[k], blocks - 1)
-            flux = get(east, coefs[k], blocks - 1) * (jnp.where(last_lane, rolled[k], pltpu.roll(v, turn, 1)) - v)
-            from_west.append(pltpu.roll(flux, 1, 1))
-
-        def body(i, carry):
-            rolled, from_west, extra = carry
-            for u in range(unroll):
-                j = i * unroll + u
-                after = j + 1
-                if u == unroll - 1:
-                    after = jnp.where(after == blocks, 0, after)
-                vs = [get(source, t, j) for t in tiles]
-                lifted = [pltpu.roll(v, 7, 0) for v in vs]
-                rise = []
-                for k in ring:
-                    above = jnp.where(last_sub, lifted[(k + 1) % len(tiles)], lifted[k])
-                    rise.append(get(north, coefs[k], j) * (above - vs[k]))
-                sunk = [pltpu.roll(f, 1, 0) for f in rise]
-                next_rolled, next_west, results = [], [], []
-                for k in ring:
-                    ahead = pltpu.roll(get(source, tiles[k], after), turn, 1)
-                    flux = get(east, coefs[k], j) * (jnp.where(last_lane, ahead, rolled[k]) - vs[k])
-                    turned = pltpu.roll(flux, 1, 1)
-                    west = jnp.where(first_lane, from_west[k], turned)
-                    south = jnp.where(first_sub, sunk[k - 1], sunk[k])
-                    result = vs[k] + ((flux - west) + (rise[k] - south))
-                    results.append(result * keep if coefs[k] == own else result)
-                    next_rolled.append(ahead)
-                    next_west.append(turned)
-                rolled, from_west = tuple(next_rolled), tuple(next_west)
-                extra = finish(j, results, extra)
-            return rolled, from_west, extra
-
-        return lax.fori_loop(0, blocks // unroll, body, (rolled, tuple(from_west), init))[2]
-
-    def into(target):
-        def finish(j, results, extra):
-            for t, result in enumerate(results):
-                target[8 * t : 8 * t + 8, block(j)] = result
-            return extra
-
-        return finish
-
-    inner = list(range(own))
-    edge = [own - 1, own, 0]
-    flat = [0, 1, 2]
     from_edge = jnp.where(low, sub, 7 - sub) < 4
 
-    diffuse(field, inner, inner, into(ping))
-    diffuse(ping, inner, inner, into(pong))
-    diffuse(pong, inner, inner, into(ping))
-    picked = diffuse(ping, inner, inner, lambda j, results, accs: pick(j, accs, results), zero_tiles)
+    def pick(t, first, second):
+        found = jnp.zeros(tile, jnp.float32)
+        for j in range(blocks):
+            got = jnp.where(low, lane_gather(first(j), los[t]), lane_gather(second(j), los[t]))
+            found = jnp.where(his[t] == j, got, found)
+        return found
+
+    def member_rows(t):
+        def rows_at(j):
+            pair = member[16 * (t // 2) : 16 * (t // 2) + 16, block(j)].astype(jnp.float32)
+            return pair[8 * (t % 2) : 8 * (t % 2) + 8]
+
+        return rows_at
+
+    def rows_of_tile(ref, t):
+        return lambda j: get(ref, t, j)
+
+    loads[7].wait()
+    for t in range(half):
+        member_at[t] = pick(t, member_rows(t), member_rows(own - 1 - t))
+    picked = [pick(t, rows_of_tile(pong, t), rows_of_tile(pong, own - 1 - t)) for t in range(half)]
     for t in range(1, half):
         part[t] = member_at[t] * picked[t]
 
@@ -330,14 +323,12 @@
         for copy in to_up:
             copy.wait_recv()
 
-    def pick_edge(j, results, acc):
-        got = jnp.where(low, lane_gather(results[2], los[0]), lane_gather(results[0], los[0]))
-        return jnp.where(his[0] == j, got, acc)
-
-    diffuse(field, edge, edge, into(edge_a))
-    diffuse(edge_a, flat, edge, into(edge_b))
-    diffuse(edge_b, flat, edge, into(edge_a))
-    picked_edge = diffuse(edge_a, flat, edge, pick_edge, zero_tiles[0])
+    west_tile(own)
+    diffuse(field, edge, edge, 1, into(edge_a))
+    diffuse(edge_a, flat, edge, 1, into(edge_b))
+    diffuse(edge_b, flat, edge, 1, into(edge_a))
+    diffuse(edge_a, flat, edge, 1, into(edge_b))
+    picked_edge = pick(0, rows_of_tile(edge_b, 2), rows_of_tile(edge_b, 0))
     part[0] = member_at[0] * jnp.where(from_edge, picked_edge, picked[0])
     send(0, 0)
 
@@ -351,7 +342,7 @@
             lanes = half_base | ((lane - d) & (per_row - 1))
             later = in_half >= d
             for t in range(half):
-                w0, w1, w2, v0, v1, v2, repeat = carry[t]
+                w0, w1, w2, v0, v1, v2, again = carry[t]
                 other = lane_gather(key_tile[t], lanes)
                 w = lane_gather(wgt_tile[t], lanes)
                 v = lane_gather(wv_tile[t], lanes)
@@ -363,7 +354,7 @@
                 carry[t] = (
                     w0 + jnp.where(m0, w, 0.0), w1 + jnp.where(m1, w, 0.0), w2 + jnp.where(m2, w, 0.0),
                     v0 + jnp.where(m0, v, 0.0), v1 + jnp.where(m1, v, 0.0), v2 + jnp.where(m2, v, 0.0),
-                    jnp.where(same & later, 1, repeat),
+                    jnp.where(same & later, 1, again),
                 )
         return tuple(carry)
 
@@ -383,29 +374,34 @@
 
     loads[8].wait()
 
-    def pick_back(j, accs):
-        return pick(j, accs, [back[8 * t : 8 * t + 8, block(j)] for t in range(own)])
-
-    for t, value in enumerate(over_blocks(pick_back)):
-        back_at[t] = value
+    for t in range(half):
+        back_at[t] = pick(t, rows_of_tile(back, t), rows_of_tile(back, own - 1 - t))
 
     for t in range(1, half):
         total = collect(t, 0)
         part[half + t] = total
         send(t, 1)
 
+    @pl.when(has_up)
+    def _():
+        cols_to_down.wait_recv()
+
+    @pl.when(has_down)
+    def _():
+        cols_to_up.wait_recv()
+
     halo_cols = jnp.where(sub < 4, col_up[...], col_down[...])
     col_tile[half] = halo_cols
 
-    def find_repeat(i, repeat):
+    def find_repeat(i, again):
         for u in range(9):
             d = 9 * i + 1 + u
             lanes = half_base | ((lane - d) & (per_row - 1))
-            repeat = jnp.where((lane_gather(halo_cols, lanes) == halo_cols) & (in_half >= d), 1, repeat)
-        return repeat
-
-    repeat = lax.fori_loop(0, (per_row - 1) // 9, find_repeat, jnp.zeros(tile, jnp.int32))
-    rep_tile[half] = jnp.where(repeat == 0, lane + 1, 0)
+            again = jnp.where((lane_gather(halo_cols, lanes) == halo_cols) & (in_half >= d), 1, again)
+        return again
+
+    again = lax.fori_loop(0, (per_row - 1) // 9, find_repeat, jnp.zeros(tile, jnp.int32))
+    rep_tile[half] = jnp.where(again == 0, lane + 1, 0)
 
     def spot(t, s):
         col = col_tile[t, pl.ds(s, 1), :]
@@ -470,22 +466,21 @@
     place_tile(0, use)
     place_tile(own - 1, use)
 
-    def to_out(j, results, extra):
-        for t in range(own):
-            out_ref[0, 8 * t : 8 * t + 8, block(j)] = results[t] + get(field, t, j)
-        return extra
-
-    def edge_out(j, results, extra):
-        for k, t, mine in ((2, 0, sub < 4), (0, own - 1, sub >= 4)):
-            rows_at = pl.ds(8 * t, 8)
-            value = jnp.where(mine, results[k] + get(field, t, j), out_ref[0, rows_at, block(j)])
-            out_ref[0, rows_at, block(j)] = value
-        return extra
-
-    diffuse(ping, inner, inner, into(pong))
-    diffuse(pong, inner, inner, into(third))
-    diffuse(third, inner, inner, into(pong))
-    diffuse(pong, inner, inner, to_out)
+    def to_out(k, j, result):
+        out_ref[0, 8 * k : 8 * k + 8, block(j)] = result + get(field, k, j)
+
+    def edge_out(k, j, result):
+        t = edge[k]
+        if t == own:
+            return
+        rows_at = slice(8 * t, 8 * t + 8)
+        mine = sub < 4 if t == 0 else sub >= 4
+        out_ref[0, rows_at, block(j)] = jnp.where(mine, result + get(field, t, j), out_ref[0, rows_at, block(j)])
+
+    diffuse(ping, inner, inner, half, into(pong))
+    diffuse(pong, inner, inner, half, into(third))
+    diffuse(third, inner, inner, half, into(pong))
+    diffuse(pong, inner, inner, half, to_out)
 
     @pl.when(has_up)
     def _():
@@ -496,10 +491,10 @@
         use_to_up.wait_recv()
 
     place_tile(own, jnp.where(sub < 4, use_up[...], use_down[...]))
-    diffuse(ping, edge, edge, into(edge_a))
-    diffuse(edge_a, flat, edge, into(edge_b))
-    diffuse(edge_b, flat, edge, into(edge_a))
-    diffuse(edge_a, flat, edge, edge_out)
+    diffuse(ping, edge, edge, 1, into(edge_a))
+    diffuse(edge_a, flat, edge, 1, into(edge_b))
+    diffuse(edge_b, flat, edge, 1, into(edge_a))
+    diffuse(edge_a, flat, edge, 1, edge_out)
 
     for of_tile in copies:
         for of_stage in of_tile:
@@ -508,12 +503,12 @@
 
     @pl.when(has_up)
     def _():
-        for copy in to_up + [use_to_up]:
+        for copy in to_up + [cols_to_up, use_to_up]:
             copy.wait_send()
 
     @pl.when(has_down)
     def _():
-        for copy in to_down + [use_to_down]:
+        for copy in to_down + [cols_to_down, use_to_down]:
             copy.wait_send()
 
 
@@ -531,7 +526,7 @@
         f32, i32 = jnp.float32, jnp.int32
         VMEM = pltpu.VMEM
         scratch = [
-            VMEM((ext, columns), f32), VMEM((ext, columns), f32), VMEM((ext, columns), f32),
+            VMEM((ext, columns), f32), VMEM((ext, columns), f32), VMEM((ext, columns), f32), VMEM((ext, columns), f32),
             VMEM((ext, columns), f32), VMEM((ext, columns), f32), VMEM((rows, columns), f32),
             VMEM((24, columns), f32), VMEM((24, columns), f32),
             VMEM((rows, columns), jnp.bfloat16), VMEM((rows, columns), f32),

time: 39.5 us -> 36.6 us (0.927)
  Pallas kernels: 38.4 us -> 35.6 us
    pallas_call x1, Pallas kernels: 38.4 us -> 35.6 us  [per_device(): pl.pallas_call(functools.partial(kernel, axes), out_shape=jax.ShapeDtypeS...]
where the time goes in v3:
time: 36.6 us; the launch traced here: 36.5 us
  Pallas kernels  35.6 us (97%)
  local copies, waits for them, and re-layouts  0.88 us (2%)
    pallas_call x1, Pallas kernels, per_device(): pl.pallas_call(functools.partial(kernel, axes), out_shape=jax.ShapeDtypeS...  35.6 us
    unnamed x1, local copies, waits for them, and re-layouts  0.88 us

profile of v3, /device:TPU:1, one launch (start us, length us, event | category | flops | bytes accessed | tf_op | source)
XLA Modules:
  0.0 36.5 jit_solution(6741340291455954015)
XLA Ops:
  0.0 35.6 %gradient.1 = f32[1,64,3072]{2,1,0:T(8,128)S(1)} custom-call(f32[1,64,3072]{2,1,0:T(8,128)} %alpha_hbm.1, bf16[1,64,3072]{2,1,0:T(8,128)(2,1)} %member_hbm.1, f32[64,3072]{1,0:T(8,128)} %back_hbm.1, f32[64,3072]{1,0:T(8,128)} %east_hbm.1, f32[64,3072]{1,0:T(8,128)} %north_hbm.1, s32[32,128]{1,0:T(8,128)} %bitcast.4, s32[32,128]{1,0:T(8,128)} %bitcast.5, ...), custom_call_target="tpu_custom_call" | custom-call | tf_op jit(solution)/shard_map/gradient/pallas_call | solution.py:543
  35.6 0.9 %copy.11 = f32[1,64,3072]{2,1,0:T(8,128)} copy(f32[1,64,3072]{2,1,0:T(8,128)S(1)} %gradient.1) | data formatting | bytes 1572864

commit v4 on v3

--- a/solution.py
+++ b/solution.py
@@ -48,7 +48,7 @@
             (value_hbm, value_raw), (weight_hbm, weight_raw), (member_hbm.at[0], member), (back_hbm, back),
         ))
     ]
-    for load in loads:
+    for load in loads[3:8] + loads[:3] + loads[8:]:
         load.start()
 
     lat = lax.axis_index("lat")
@@ -205,15 +205,6 @@
     edge = [own - 1, own, 0]
     flat = [0, 1, 2]
 
-    for load in loads[:3]:
-        load.wait()
-    for t in range(own):
-        west_tile(t)
-    diffuse(field, inner, inner, half, into(ping))
-    diffuse(ping, inner, inner, half, into(pong))
-    diffuse(pong, inner, inner, half, into(ping))
-    diffuse(ping, inner, inner, half, into(pong))
-
     def to_tiles(raw):
         rows_of = rows_int if raw.dtype == jnp.int32 else rows_float
         rows_of[pl.ds(0, rows // 2, stride=2), :] = raw
@@ -275,6 +266,15 @@
     loads[7].wait()
     for t in range(half):
         member_at[t] = pick(t, member_rows(t), member_rows(own - 1 - t))
+    for load in loads[:3]:
+        load.wait()
+    for t in range(own):
+        west_tile(t)
+    diffuse(field, inner, inner, half, into(ping))
+    diffuse(ping, inner, inner, half, into(pong))
+    diffuse(pong, inner, inner, half, into(ping))
+    diffuse(ping, inner, inner, half, into(pong))
+
     picked = [pick(t, rows_of_tile(pong, t), rows_of_tile(pong, own - 1 - t)) for t in range(half)]
     for t in range(1, half):
         part[t] = member_at[t] * picked[t]
@@ -327,7 +327,8 @@
     diffuse(field, edge, edge, 1, into(edge_a))
     diffuse(edge_a, flat, edge, 1, into(edge_b))
     diffuse(edge_b, flat, edge, 1, into(edge_a))
-    diffuse(edge_a, flat, edge, 1, into(edge_b))
+    last = into(edge_b)
+    diffuse(edge_a, flat, edge, 1, lambda k, j, result: None if k == 1 else last(k, j, result))
     picked_edge = pick(0, rows_of_tile(edge_b, 2), rows_of_tile(edge_b, 0))
     part[0] = member_at[0] * jnp.where(from_edge, picked_edge, picked[0])
     send(0, 0)
@@ -377,11 +378,6 @@
     for t in range(half):
         back_at[t] = pick(t, rows_of_tile(back, t), rows_of_tile(back, own - 1 - t))
 
-    for t in range(1, half):
-        total = collect(t, 0)
-        part[half + t] = total
-        send(t, 1)
-
     @pl.when(has_up)
     def _():
         cols_to_down.wait_recv()
@@ -402,6 +398,14 @@
 
     again = lax.fori_loop(0, (per_row - 1) // 9, find_repeat, jnp.zeros(tile, jnp.int32))
     rep_tile[half] = jnp.where(again == 0, lane + 1, 0)
+
+    def forward(t):
+        part[half + t] = collect(t, 0)
+        send(t, 1)
+
+    for t in (2, 0, 1, 3):
+        if t < half:
+            forward(t)
 
     def spot(t, s):
         col = col_tile[t, pl.ds(s, 1), :]
@@ -425,9 +429,6 @@
         return carry
 
     lax.fori_loop(0, 4, all_rows, 0)
-
-    part[half] = collect(0, 0)
-    send(0, 1)
 
     def use_of(t):
         s = back_at[t] + collect(t, 1)

time: 36.6 us -> 35.7 us (0.975)
  Pallas kernels: 35.6 us -> 34.7 us
    pallas_call x1, Pallas kernels: 35.6 us -> 34.7 us  [per_device(): pl.pallas_call(functools.partial(kernel, axes), out_shape=jax.ShapeDtypeS...]
where the time goes in v4:
time: 35.7 us; the launch traced here: 35.6 us
  Pallas kernels  34.7 us (97%)
  local copies, waits for them, and re-layouts  0.88 us (2%)
    pallas_call x1, Pallas kernels, per_device(): pl.pallas_call(functools.partial(kernel, axes), out_shape=jax.ShapeDtypeS...  34.7 us
    unnamed x1, local copies, waits for them, and re-layouts  0.88 us

profile of v4, /device:TPU:1, one launch (start us, length us, event | category | flops | bytes accessed | tf_op | source)
XLA Modules:
  0.0 35.6 jit_solution(2347566715923824309)
XLA Ops:
  0.0 34.7 %gradient.1 = f32[1,64,3072]{2,1,0:T(8,128)S(1)} custom-call(f32[1,64,3072]{2,1,0:T(8,128)} %alpha_hbm.1, bf16[1,64,3072]{2,1,0:T(8,128)(2,1)} %member_hbm.1, f32[64,3072]{1,0:T(8,128)} %back_hbm.1, f32[64,3072]{1,0:T(8,128)} %east_hbm.1, f32[64,3072]{1,0:T(8,128)} %north_hbm.1, s32[32,128]{1,0:T(8,128)} %bitcast.4, s32[32,128]{1,0:T(8,128)} %bitcast.5, ...), custom_call_target="tpu_custom_call" | custom-call | tf_op jit(solution)/shard_map/gradient/pallas_call | solution.py:544
  34.8 0.9 %copy.11 = f32[1,64,3072]{2,1,0:T(8,128)} copy(f32[1,64,3072]{2,1,0:T(8,128)S(1)} %gradient.1) | data formatting | bytes 1572864
